TPU v7x, 32 devices: a whole 2x2x4 slice. The times are simulated.
32 devices in a mesh: dp: 32 (over z, y, x, core).
Axes of the slice: x: 2, y: 2, z: 4, core: 2. Of those that a mesh axis runs over, the one named last changes fastest.
Arguments:
- text_states: bfloat16 [512, 16, 768], P('dp'), may hold values from -6 to 6
- text_len: int32 [512], P('dp'), may hold values from 1 to 16
- query_states: bfloat16 [512, 16, 768], P('dp'), may hold values from -6 to 6
- neg_owner: int32 [512, 2], P('dp'), may hold values from 0 to 31, all different within a row; in each aligned block of 16 rows (0 to 15, 16 to 31, ...) at most 2 rows name the same one
- neg_slot: int32 [512, 2], P('dp'), may hold values from 0 to 15
- projection_weight: bfloat16 [768, 2304], replicated, may hold values from -0.21875 to 0.21875
- output_weight: bfloat16 [768, 768], replicated, may hold values from -0.21875 to 0.21875
- ln_gain: float32 [768], replicated, may hold values from 0.5 to 1.5
- ln_bias: float32 [768], replicated, may hold values from -3 to 3
- itm_weight: float32 [768, 2], replicated, may hold values from -0.875 to 0.875
- itm_bias: float32 [2], replicated, may hold values from -3 to 3
Outputs:
- pair_logits: float32 [512, 3, 2], P('dp')
- grad_text: bfloat16 [512, 16, 768], P('dp')
- grad_query: bfloat16 [512, 16, 768], P('dp')
- grad_qkv: float32 [768, 2304], replicated
- grad_out: float32 [768, 768], replicated
Inputs may be any that keep to these rules, and one draw needn't show every extreme that they name: `neg_owner`: the two negatives of a caption lie in different blocks; among the 16 captions of one device no block is named more than 2 times, and in some device exactly 2 times.
All inputs are finite; a program needn't handle non-finite values.
Results may differ from a plain program's by a relative error of at most 0.0075.
Values may be sent and summed in bfloat16 or wider, within the bound.
No kernel may reach another device: no remote copies, remote signals or barrier semaphores. Data moves between devices by JAX's collectives and lax.ppermute only.
A program may use at most 128 MiB of HBM per device.

v0:
```python
import functools
import jax
import jax.numpy as jnp
from jax import lax
from jax.experimental import pallas as pl
from jax.experimental.pallas import tpu as pltpu

from jax.sharding import PartitionSpec as P


BF = jnp.bfloat16
F32 = jnp.float32


def dot_nt(a, b):
    return lax.dot_general(a, b, (((1,), (1,)), ((), ())), preferred_element_type=F32)


def dot_nn(a, b):
    return lax.dot_general(a, b, (((1,), (0,)), ((), ())), preferred_element_type=F32)


def core_kernel(lens, source, w_h, tkv, wo_h, gain, bias, head_w, head_b, text_h, place, logits, x_h, ga_h, ctx_h, dqkv_h, dtext_h, back_h, qkv, probs, dctx, gh, w, wo, text_in, x, ga, ctx, dqkv, dtext, back, sem_in, sem_out, sem_rows, *, positive):
    rows, width = ctx.shape
    loads = [
        pltpu.make_async_copy(
            w_h.at[:, pl.ds(n * width, width)], w.at[:, pl.ds(n * width, width)], sem_in.at[n]
        )
        for n in range(3)
    ]
    loads.append(pltpu.make_async_copy(wo_h, wo, sem_in.at[3]))
    if not positive:
        loads.append(pltpu.make_async_copy(text_h, text_in, sem_in.at[4]))
    for load in loads:
        load.start()
    saves = []

    def save(src, dst):
        copy = pltpu.make_async_copy(src, dst, sem_out.at[len(saves)])
        copy.start()
        saves.append(copy)

    pairs_of_units = rows // 64
    quads = width // 256
    scale = 0.125
    lane = lax.broadcasted_iota(jnp.int32, (128, 128), 1)
    left = lane < 64
    lane32 = lax.broadcasted_iota(jnp.int32, (32, 128), 1)
    row32 = lax.broadcasted_iota(jnp.int32, (32, 128), 0)
    qg = row32 // 16
    uu = lane32 // 64
    key = lane32 % 64
    is_image = key < 32
    image_ok = is_image & ((key // 16) == qg)
    tg = (key - 32) // 16
    tpos = key % 16
    text_ok = jnp.logical_not(is_image) & (tg == qg)
    half32 = lane32 < 64
    hm_lane = lax.broadcasted_iota(jnp.int32, (1, 256), 1) // 64
    head_mask = [(hm_lane == h).astype(F32).astype(BF) for h in range(4)]
    zero64 = jnp.zeros((64, 256), BF)

    def head_blocks(t):
        return jnp.concatenate([t * m for m in head_mask], axis=0)

    def unit_rows(j, u):
        return pl.ds(pl.multiple_of(j * 64 + u * 32, 32), 32)

    def stacked(j, part, q):
        cols = pl.ds(width * part + q * 256, 256)
        tcols = pl.ds(width * (part - 1) + q * 256, 256)
        both = []
        for u in range(2):
            t = jnp.concatenate([qkv[unit_rows(j, u), cols], tkv[unit_rows(j, u), tcols]], axis=0)
            both.append(t)
        return jnp.concatenate(
            [jnp.concatenate([both[0], zero64], axis=1), jnp.concatenate([zero64, both[1]], axis=1)],
            axis=0,
        )

    def wide(ref, j, q):
        cols = pl.ds(q * 256, 256)
        return [head_blocks(ref[unit_rows(j, u), cols]) for u in range(2)]

    def gathered(full, u):
        parts = []
        for t in range(2):
            cols = slice(u * 256 + t * 128, u * 256 + t * 128 + 128)
            a = full[(2 * t) * 32 : (2 * t + 1) * 32, cols]
            b = full[(2 * t + 1) * 32 : (2 * t + 2) * 32, cols]
            parts.append(jnp.where(half32, a, b))
        return jnp.concatenate(parts, axis=1)

    def half_reduce(t, fill, op):
        a = op(jnp.where(left, t, fill), axis=1, keepdims=True)
        b = op(jnp.where(left, fill, t), axis=1, keepdims=True)
        return a, b

    def forward(j, carry):
        n = [lens[4 * j + i] for i in range(4)]
        limit = jnp.where(
            uu == 0, jnp.where(qg == 0, n[0], n[1]), jnp.where(qg == 0, n[2], n[3])
        )
        valid32 = image_ok | (text_ok & (tpos < limit))
        valid32 = jnp.where(valid32, 1.0, 0.0)
        valid = jnp.concatenate([valid32] * 4, axis=0) > 0.5
        for q in range(quads):
            queries = wide(qkv, j, q)
            keys = stacked(j, 1, q)
            s = dot_nt(jnp.concatenate(queries, axis=1), keys) * scale
            s = jnp.where(valid, s, -1e30)
            m0, m1 = half_reduce(s, -3e38, jnp.max)
            e = jnp.exp(s - jnp.where(left, m0, m1))
            d0, d1 = half_reduce(e, 0.0, jnp.sum)
            p = e * jnp.where(left, 1.0 / d0, 1.0 / d1)
            probs[j, q] = p
            full = dot_nn(p.astype(BF), stacked(j, 2, q))
            for u in range(2):
                ctx[unit_rows(j, u), pl.ds(q * 256, 256)] = gathered(full, u).astype(BF)
        return carry

    if positive:
        x = source
    else:
        for i in range(rows // 16):
            x[i * 16 : i * 16 + 16, :] = source[pl.ds(pl.multiple_of(place[i] * 16, 16), 16), :]
        save(x, x_h)

    def project(n, carry):
        cols = pl.ds(pl.multiple_of(n * 256, 256), 256)
        qkv[:, cols] = dot_nn(x[...], w[:, cols]).astype(BF)
        return carry

    per = width // 256
    for n in range(3):
        loads[n].wait()
        lax.fori_loop(n * per, (n + 1) * per, project, 0)
    lax.fori_loop(0, pairs_of_units, forward, 0)
    save(ctx, ctx_h)
    loads[3].wait()

    chunk = 128
    w0 = head_w[0:1, :]
    w1 = head_w[1:2, :]

    def middle(i, carry):
        rs = pl.ds(pl.multiple_of(i * chunk, chunk), chunk)
        hid = x[rs, :].astype(F32) + dot_nn(ctx[rs, :], wo[...])
        cen = hid - jnp.mean(hid, axis=1, keepdims=True)
        spread = jnp.mean(cen * cen, axis=1, keepdims=True)
        inv = lax.rsqrt(spread + 1e-06)
        xhat = cen * inv
        pooled = jnp.sum(xhat.reshape(chunk // 16, 16, width), axis=1) * (1.0 / 16.0)
        pooled = pooled * gain[...] + bias[...]
        l0 = jnp.sum(pooled * w0, axis=1, keepdims=True) + head_b[0]
        l1 = jnp.sum(pooled * w1, axis=1, keepdims=True) + head_b[1]
        cols = lax.broadcasted_iota(jnp.int32, (chunk // 16, 128), 1)
        logits[pl.ds(pl.multiple_of(i * (chunk // 16), chunk // 16), chunk // 16), :] = jnp.where(
            cols == 0, l0, l1
        )
        top = jnp.maximum(l0, l1)
        e0 = jnp.exp(l0 - top)
        e1 = jnp.exp(l1 - top)
        wrong = (e0 if positive else e1) / (e0 + e1)
        slope = (w0 - w1) if positive else (w1 - w0)
        dx = (wrong * (1.0 / 16.0)) * slope * gain[...]
        mean_dx = jnp.mean(dx, axis=1, keepdims=True)
        dx = jnp.broadcast_to(dx[:, None, :], (chunk // 16, 16, width)).reshape(chunk, width)
        mean_dx = jnp.broadcast_to(mean_dx[:, None, :], (chunk // 16, 16, 1)).reshape(chunk, 1)
        along = jnp.mean(dx * xhat, axis=1, keepdims=True)
        g = inv * (dx - mean_dx - xhat * along)
        gh[rs, :] = g
        gl = g.astype(BF)
        ga[rs, :] = gl
        dctx[rs, :] = dot_nt(gl, wo[...]).astype(BF)
        return carry

    lax.fori_loop(0, rows // chunk, middle, 0)
    save(ga, ga_h)
    if not positive:
        loads[4].wait()

    def row_copies(j):
        rs = pl.ds(pl.multiple_of(j * 64, 64), 64)
        return [
            pltpu.make_async_copy(dqkv.at[rs, :], dqkv_h.at[rs, :], sem_rows.at[0, j]),
            pltpu.make_async_copy(dtext.at[rs, :], dtext_h.at[rs, :], sem_rows.at[1, j]),
        ]

    def backward(j, carry):
        for q in range(quads):
            p = probs[j, q]
            dc = wide(dctx, j, q)
            dp = dot_nt(jnp.concatenate(dc, axis=1), stacked(j, 2, q))
            r0, r1 = half_reduce(dp * p, 0.0, jnp.sum)
            ds = (p * (dp - jnp.where(left, r0, r1)) * scale).astype(BF)
            full = dot_nn(ds, stacked(j, 1, q))
            for u in range(2):
                dqkv[unit_rows(j, u), pl.ds(q * 256, 256)] = gathered(full, u).astype(BF)
            queries = wide(qkv, j, q)
            dst = ds.T
            pt = p.astype(BF).T
            for part, lhs, rhs in ((1, dst, queries), (2, pt, dc)):
                outs = [dot_nn(lhs[u * 64 : u * 64 + 64], rhs[u]) for u in range(2)]
                for u in range(2):
                    dqkv[unit_rows(j, u), pl.ds(width * part + q * 256, 256)] = outs[u][:32].astype(BF)
                tcols = pl.ds(width * (part - 1) + q * 256, 256)
                for u in range(2):
                    total = outs[u][32:]
                    if not positive:
                        total = total + text_in[unit_rows(j, u), tcols]
                    dtext[unit_rows(j, u), tcols] = total.astype(dtext.dtype)
        for copy in row_copies(j):
            copy.start()
        return carry

    lax.fori_loop(0, pairs_of_units, backward, 0)

    def images(n, carry):
        cols = pl.ds(pl.multiple_of(n * 256, 256), 256)
        g = dot_nt(dqkv[...], w[cols, :]) + gh[:, cols]
        if positive:
            back[:, cols] = g
        else:
            gh[:, cols] = g
        return carry

    lax.fori_loop(0, width // 256, images, 0)
    if not positive:
        back[...] = jnp.zeros(back.shape, BF)
        for i in range(rows // 16):
            at = pl.ds(pl.multiple_of(place[i] * 16, 16), 16)
            back[at, :] = gh[i * 16 : i * 16 + 16, :].astype(BF)
    save(back, back_h)
    for j in range(pairs_of_units):
        for copy in row_copies(j):
            copy.wait()
    for copy in saves:
        copy.wait()


def pair_core(text_type, lens, source, w, tkv, wo, gain, bias, head_w, head_b, text_in, place):
    rows, width = tkv.shape[0], wo.shape[0]
    positive = place is None
    vm = pl.BlockSpec(memory_space=pltpu.VMEM)
    sm = pl.BlockSpec(memory_space=pltpu.SMEM)
    far = pl.BlockSpec(memory_space=pl.ANY)
    ins = [lens, source, w, tkv, wo, gain, bias, head_w, head_b]
    specs = [sm, vm, far, vm, far, vm, vm, vm, sm]
    if not positive:
        ins += [text_in, place]
        specs += [far, sm]
    back_type = F32 if positive else BF
    shapes = [
        ((rows, width), BF),
        ((rows, width), BF),
        ((rows, width), BF),
        ((rows, 3 * width), BF),
        ((rows, 2 * width), text_type),
        (source.shape, back_type),
    ]
    out = [jax.ShapeDtypeStruct((rows // 16, 128), F32)]
    out += [jax.ShapeDtypeStruct(s, t) for s, t in shapes]
    if positive:
        del out[1]

    def body(*refs):
        if positive:
            refs = refs[:9] + (None, None, refs[9], None) + refs[10:]
        core_kernel(*refs, positive=positive)

    units = rows // 64
    result = pl.pallas_call(
        body,
        out_shape=out,
        in_specs=specs,
        out_specs=[vm] + [far] * (len(out) - 1),
        scratch_shapes=[
            pltpu.VMEM((rows, 3 * width), BF),
            pltpu.VMEM((units, width // 256, 128, 128), F32),
            pltpu.VMEM((rows, width), BF),
            pltpu.VMEM((rows, width), F32),
            pltpu.VMEM(w.shape, BF),
            pltpu.VMEM(wo.shape, BF),
            pltpu.VMEM((rows, 2 * width), F32),
            *[pltpu.VMEM(s, t) for s, t in shapes],
            pltpu.SemaphoreType.DMA((5,)),
            pltpu.SemaphoreType.DMA((4,)),
            pltpu.SemaphoreType.DMA((2, units)),
        ],
        name="pair_core",
        compiler_params=pltpu.CompilerParams(vmem_limit_bytes=56 * 1024 * 1024),
    )(*ins)
    if positive:
        return [result[0], source] + list(result[1:])
    return result


def give_kernel(wanted, images, first, second):
    for p in range(first.shape[0] // 16):
        for s, out in enumerate((first, second)):
            at = jnp.maximum(wanted[p, s] - 1, 0)
            out[p * 16 : p * 16 + 16, :] = images[pl.ds(pl.multiple_of(at * 16, 16), 16), :]


def give(wanted, images):
    vm = pl.BlockSpec(memory_space=pltpu.VMEM)
    shape = jax.ShapeDtypeStruct((wanted.shape[0] * 16, images.shape[1]), BF)
    return pl.pallas_call(
        give_kernel,
        out_shape=[shape, shape],
        in_specs=[pl.BlockSpec(memory_space=pltpu.SMEM), vm],
        out_specs=[vm, vm],
        name="give",
    )(wanted, images)


def receive_kernel(wanted, own, first, second, out, total):
    total[...] = own[...]
    for s, part in enumerate((first, second)):

        def add(p, carry):
            at = wanted[p, s]

            @pl.when(at > 0)
            def _():
                rows = pl.ds(pl.multiple_of((at - 1) * 16, 16), 16)
                src = part[pl.ds(pl.multiple_of(p * 16, 16), 16), :]
                total[rows, :] = total[rows, :] + src.astype(F32)

            return carry

        lax.fori_loop(0, first.shape[0] // 16, add, 0)
    out[...] = total[...].astype(BF)


def receive(wanted, own, first, second):
    vm = pl.BlockSpec(memory_space=pltpu.VMEM)
    return pl.pallas_call(
        receive_kernel,
        out_shape=jax.ShapeDtypeStruct(own.shape, BF),
        in_specs=[pl.BlockSpec(memory_space=pltpu.SMEM), vm, vm, vm],
        out_specs=vm,
        scratch_shapes=[pltpu.VMEM(own.shape, F32)],
        name="receive",
    )(wanted, own, first, second)


def route_kernel(owner, slot, wanted, owners, color0):
    count = owner.shape[0]
    n = 2 * count
    peers = wanted.shape[0]
    o0, o1 = owner[:, 0:1], owner[:, 1:2]
    i = lax.broadcasted_iota(jnp.int32, (n, n), 0)
    k = lax.broadcasted_iota(jnp.int32, (n, n), 1)
    i_swap = jnp.where(i < count, i + count, i - count)
    k_swap = jnp.where(k < count, k + count, k - count)

    def row_of(col):
        return jnp.sum(jnp.where(i == k, col, 0), axis=0, keepdims=True)

    owner_col = jnp.concatenate([o0, o1], axis=0)
    swap_col = jnp.concatenate([o1, o0], axis=0)
    owner_row = row_of(owner_col)
    swap_row = row_of(swap_col)
    slot_row = row_of(jnp.concatenate([slot[:, 0:1], slot[:, 1:2]], axis=0))
    ahead = (owner_col == swap_row) & (i != k_swap)
    behind = (owner_row == swap_col) & (k != i_swap)
    reach = jnp.where(ahead | behind | (i == k), 1.0, 0.0)
    span = 1
    while span < count:
        low = reach.astype(BF)
        reach = jnp.where(dot_nn(low, low) > 0.5, 1.0, 0.0)
        span *= 2
    near = reach > 0.5
    first_row = jnp.min(jnp.where(near, i, n), axis=0, keepdims=True)
    second_row = jnp.min(jnp.where(near, i_swap, n), axis=0, keepdims=True)
    color_row = jnp.where(first_row < second_row, 0, 1)
    peer = lax.broadcasted_iota(jnp.int32, (peers, n), 0)
    asked = []
    for s in range(2):
        hit = (owner_row == peer) & (color_row == s)
        asked.append(jnp.sum(jnp.where(hit, slot_row + 1, 0), axis=1, keepdims=True))
    wanted[...] = jnp.concatenate(asked, axis=1)
    own_color = color_row[:, :count]
    swapped = owner_row[:, count:]
    straight = owner_row[:, :count]
    color0[...] = own_color
    owners[...] = jnp.concatenate(
        [jnp.where(own_color == 0, straight, swapped), jnp.where(own_color == 0, swapped, straight)],
        axis=0,
    )


def route(owner, slot, peers):
    vm = pl.BlockSpec(memory_space=pltpu.VMEM)
    count = owner.shape[0]
    return pl.pallas_call(
        route_kernel,
        out_shape=[
            jax.ShapeDtypeStruct((peers, 2), jnp.int32),
            jax.ShapeDtypeStruct((2, count), jnp.int32),
            jax.ShapeDtypeStruct((1, count), jnp.int32),
        ],
        in_specs=[vm, vm],
        out_specs=[vm, vm, vm],
        name="route",
    )(owner, slot)


def weight_kernel(core, *refs, flips, groups, with_text):
    xs = refs[:groups]
    ds = refs[groups : 2 * groups]
    rest = refs[2 * groups :]
    if with_text:
        text, dt = rest[:2]
        rest = rest[2:]
        lhs = xs + (text,)
    else:
        lhs = xs
    outs = rest[: len(flips)]
    turned = rest[len(flips) :]
    step = pl.program_id(0)
    rows_of, width = xs[0].shape
    half = width // 2
    per = width // 256
    for flip, out, hold in zip(flips, outs, turned):
        for part in range(2):

            @pl.when((step == 0) & ((core[0] + flip) % 2 == part))
            def _():
                col = 0
                for src in lhs:
                    for i in range(src.shape[0] // 128):
                        block = src[i * 128 : i * 128 + 128, part * half : (part + 1) * half]
                        hold[:, col : col + 128] = block.T
                        col += 128

        def columns(n, carry, more):
            cols = pl.ds(pl.multiple_of(n * 256, 256), 256)
            acc = dot_nn(hold[:, :rows_of], ds[0][:, cols])
            for g in range(1, groups):
                acc = acc + dot_nn(hold[:, g * rows_of : (g + 1) * rows_of], ds[g][:, cols])
            if more:
                acc = acc + dot_nn(hold[:, groups * rows_of :], dt[:, cols])
            out[:, cols] = acc.astype(BF)
            return carry

        if with_text:

            @pl.when(step == 0)
            def _():
                lax.fori_loop(0, per, functools.partial(columns, more=False), 0)

            @pl.when(step > 0)
            def _():
                lax.fori_loop(0, per, functools.partial(columns, more=True), 0)

        else:
            lax.fori_loop(0, per, functools.partial(columns, more=False), 0)


def weight_gradients(core, flips, xs, ds, text, dt):
    groups = len(xs)
    with_text = text is not None
    rows_of, width = xs[0].shape
    whole = lambda t: pl.BlockSpec(t.shape, lambda n, core: (0, 0))
    specs = [whole(x) for x in xs]
    specs += [pl.BlockSpec((rows_of, width), lambda n, core: (0, n)) for d in ds]
    arrays = [*xs, *ds]
    depth = groups * rows_of
    if with_text:
        arrays += [text, dt]
        specs.append(whole(text))
        specs.append(
            pl.BlockSpec((text.shape[0], width), lambda n, core: (0, jnp.maximum(n - 1, 0)))
        )
        depth += text.shape[0]
    half = width // 2
    return pl.pallas_call(
        functools.partial(weight_kernel, flips=flips, groups=groups, with_text=with_text),
        grid_spec=pltpu.PrefetchScalarGridSpec(
            num_scalar_prefetch=1,
            grid=(ds[0].shape[1] // width,),
            in_specs=specs,
            out_specs=[pl.BlockSpec((half, width), lambda n, core: (0, n))] * len(flips),
            scratch_shapes=[pltpu.VMEM((half, depth), BF)] * len(flips),
        ),
        out_shape=[jax.ShapeDtypeStruct((half, ds[0].shape[1]), BF)] * len(flips),
        name="weight_gradients",
        compiler_params=pltpu.CompilerParams(vmem_limit_bytes=56 * 1024 * 1024),
    )(core, *arrays)


def finish_kernel(at, part, *refs, factor):
    refs[-1][...] = part[...].astype(F32) * factor


def finish(at, part, rows, factor, before):
    count, total = part.shape
    steps = 2 if count % 32 == 0 else 1
    block = count // steps
    given = [] if before is None else [before]
    return pl.pallas_call(
        functools.partial(finish_kernel, factor=factor),
        grid_spec=pltpu.PrefetchScalarGridSpec(
            num_scalar_prefetch=1,
            grid=(steps,),
            in_specs=[pl.BlockSpec((block, total), lambda i, at: (i, 0))]
            + [pl.BlockSpec(memory_space=pl.ANY)] * len(given),
            out_specs=pl.BlockSpec((block, total), lambda i, at: (at[0] * steps + i, 0)),
        ),
        out_shape=jax.ShapeDtypeStruct((rows, total), F32),
        input_output_aliases={2: 0} if given else {},
        name="finish",
    )(at.reshape(1), part, *given)


def grid_of(mesh):
    flat = list(mesh.devices.flat)
    sizes = [len({d.coords[a] for d in flat}) for a in range(3)]
    dims, stride = [], 1
    for s in [len(flat) // (sizes[0] * sizes[1] * sizes[2])] + sizes:
        dims.append((stride, s))
        stride *= s
    return dims


def coord(dim):
    return (lax.axis_index("dp") // dim[0]) % dim[1]


def by_core(even, odd):
    if even == odd:
        return coord(even)
    return jnp.where(lax.axis_index("dp") % 2 == 0, coord(even), coord(odd))


def shifted(x, dims, k):
    n = lax.axis_size("dp")
    table = []
    for i in range(n):
        stride, size = dims[i % 2]
        c = (i // stride) % size
        table.append((i, i + ((c + k) % size - c) * stride))
    return lax.ppermute(x, "dp", table)


def total_of(terms):
    total = terms[0].astype(F32)
    for t in terms[1:]:
        total = total + t.astype(F32)
    return total


def scatter_terms(terms, dims):
    size = dims[0][1]
    at = by_core(*dims)
    split = [t.reshape((size, t.shape[0] // size) + t.shape[1:]) for t in terms]
    pick = lambda k: [
        lax.dynamic_index_in_dim(t, (at + k) % size, 0, keepdims=False) for t in split
    ]
    got = [shifted(total_of(pick(k)).astype(BF), dims, k) for k in range(1, size)]
    return pick(0) + got


def gather_rows(x, dims):
    size = dims[0][1]
    at = by_core(*dims)
    if size == 2:
        got = shifted(x, dims, 1)
        low = at == 0
        return jnp.concatenate([jnp.where(low, x, got), jnp.where(low, got, x)], axis=0)
    out = jnp.zeros((size,) + x.shape, x.dtype)
    out = lax.dynamic_update_index_in_dim(out, x, at, 0)
    for k in range(1, size):
        out = lax.dynamic_update_index_in_dim(out, shifted(x, dims, k), (at - k) % size, 0)
    return out.reshape((size * x.shape[0],) + x.shape[1:])


def step(
    text_states,
    text_len,
    query_states,
    neg_owner,
    neg_slot,
    projection_weight,
    output_weight,
    ln_gain,
    ln_bias,
    itm_weight,
    itm_bias,
    *,
    dims,
):
    captions, text_rows, width = text_states.shape
    image_rows = query_states.shape[1]
    peers = lax.axis_size("dp")
    wanted, owners, color = route(neg_owner, neg_slot, peers)
    requested = lax.all_to_all(wanted, "dp", split_axis=0, concat_axis=0, tiled=True)

    def exchange(t):
        split = t.reshape(peers, 1, image_rows, width)
        moved = lax.all_to_all(split, "dp", split_axis=0, concat_axis=0, tiled=True)
        return moved.reshape(t.shape)

    text = text_states.reshape(captions * text_rows, width)
    own = query_states.reshape(captions * image_rows, width)
    outgoing = give(requested, own)
    fetched = []
    for s in range(2):
        fetched.append(exchange(outgoing[s]))
    text_kv = dot_nn(text, projection_weight[:, width:]).astype(BF)
    results = []
    returned = []
    dtext = None
    for s in range(3):
        result = pair_core(
            BF if s == 2 else F32,
            text_len,
            own if s == 0 else fetched[s - 1],
            projection_weight,
            text_kv,
            output_weight,
            ln_gain[None],
            ln_bias[None],
            itm_weight.T,
            itm_bias,
            dtext,
            None if s == 0 else owners[s - 1],
        )
        results.append(result)
        dtext = result[5]
        if s > 0:
            returned.append(exchange(result[6]))

    rows = [r[1] for r in results]
    core = coord(dims[0]).reshape(1)
    core_dims = (dims[0], dims[0])
    x_dim, y_dim, z_dim = dims[1:]
    mixed = x_dim[1] == y_dim[1]
    flat_first = (x_dim, y_dim) if mixed else (x_dim, x_dim)
    flat_second = (y_dim, x_dim) if mixed else (y_dim, y_dim)
    deep = (z_dim, z_dim)
    factor = 1.0 / (captions * peers)

    keep_a, send_a = weight_gradients(
        core, (0, 1), [r[3] for r in results], [r[2] for r in results], None, None
    )
    a = [keep_a, shifted(send_a, core_dims, 1)]
    dqs = [r[4] for r in results]
    (send_b,) = weight_gradients(core, (1,), rows, dqs, text, dtext)
    got_b = shifted(send_b, core_dims, 1)
    (keep_b,) = weight_gradients(core, (0,), rows, dqs, text, dtext)
    b = [keep_b, got_b]
    grad_text = dot_nt(dtext, projection_weight[:, width:]).astype(BF)

    heads = [r[0][:, :2] for r in results]
    straight = color.reshape(captions, 1) == 0
    logits = jnp.stack(
        [
            heads[0],
            jnp.where(straight, heads[1], heads[2]),
            jnp.where(straight, heads[2], heads[1]),
        ],
        axis=1,
    )

    a = scatter_terms(a, deep)
    b = scatter_terms(b, flat_first)
    b = scatter_terms(b, flat_second)
    a = scatter_terms(a, flat_first)
    b = scatter_terms(b, deep)
    a = scatter_terms(a, flat_second)
    a = total_of(a).astype(BF)
    b = total_of(b).astype(BF)
    b = gather_rows(b, deep)
    a = gather_rows(a, flat_second)
    a = gather_rows(a, flat_first)
    b = gather_rows(b, flat_second)
    a = gather_rows(a, deep)
    other_a = shifted(a, core_dims, 1)
    size = flat_first[0][1]
    at = by_core(*flat_first)
    other_at = by_core(flat_first[1], flat_first[0])
    pieces = [(core[0] * size + at, b)]
    pieces.append(((1 - core[0]) * size + other_at, shifted(b, core_dims, 1)))
    for k in range(1, size):
        got = shifted(b, flat_first, k)
        pieces.append((core[0] * size + (at - k) % size, got))
        got = shifted(got, core_dims, 1)
        pieces.append(((1 - core[0]) * size + (other_at - k) % size, got))
    grad_query = receive(requested, results[0][6], *returned)
    sum_qkv = None
    for place, piece in pieces:
        sum_qkv = finish(place, piece, width, factor, sum_qkv)
    sum_out = finish(core[0], a, width, factor, None)
    sum_out = finish(1 - core[0], other_a, width, factor, sum_out)
    return (
        logits,
        grad_text.reshape(captions, text_rows, width),
        grad_query.reshape(captions, image_rows, width),
        sum_qkv,
        sum_out,
    )


def solution(mesh):
    dims = grid_of(mesh)
    placed = (
        P("dp", None, None),
        P("dp"),
        P("dp", None, None),
        P("dp", None),
        P("dp", None),
        P(),
        P(),
        P(),
        P(),
        P(),
        P(),
    )
    return jax.shard_map(
        functools.partial(step, dims=dims),
        mesh=mesh,
        in_specs=placed,
        out_specs=(P("dp", None, None), P("dp", None, None), P("dp", None, None), P(), P()),
        check_vma=False,
    )
```

profile of v0, /device:TPU:0, one launch (start us, length us, event | category | flops | bytes accessed | tf_op | source)
XLA Modules:
  0.0 274.9 jit_solution(51779490752734683)
XLA Ops:
  5.4 14.4 %all_to_all.31 = s32[32,1,2]{2,1,0:T(1,128)S(1)} all-to-all(s32[32,1,2]{2,1,0:T(1,128)} %bitcast.177), channel_id=1, replica_groups=mesh['dp'=32] {'dp'}, dimensions={0} | all-to-all | bytes 512 | tf_op jit(solution)/shard_map/all_to_all | solution.py:600
  20.6 2.4 give.1
  23.0 23.9 %all_to_all.32 = bf16[32,1,16,768]{3,2,1,0:T(8,128)(2,1)} all-to-all(bf16[32,1,16,768]{3,2,1,0:T(8,128)(2,1)} %bitcast.146), channel_id=1, replica_groups=mesh['dp'=32] {'dp'}, dimensions={0} | all-to-all | bytes 1572864 | tf_op jit(solution)/shard_map/all_to_all | solution.py:604
  46.9 3.7 %all-to-all-start.2 = ((bf16[32,1,16,768]{3,2,1,0:T(8,128)(2,1)}), bf16[32,1,16,768]{3,2,1,0:T(8,128)(2,1)}, u32[]{:S(2)}, u32[]{:S(2)}) async-start(bf16[32,1,16,768]{3,2,1,0:T(8,128)(2,1)} %bitcast.145), calls=%async_computation.2 | async-start | bytes 1572864 | tf_op jit(solution)/shard_map/all_to_all | solution.py:604
  51.8 2.7 convolution_convert_fusion.refs_3_
  54.5 19.7 %pair_core.3 = (f32[16,128]{1,0:T(8,128)}, bf16[256,768]{1,0:T(8,128)(2,1)}, bf16[256,768]{1,0:T(8,128)(2,1)}, bf16[256,2304]{1,0:T(8,128)(2,1)}, f32[256,1536]{1,0:T(8,128)}, /*index=5*/f32[256,768]{1,0:T(8,128)}) custom-call(s32[16]{0:T(128)} %refs_0_.5, bf16[256,768]{1,0:T(8,128)(2,1)} %bitcast.121, bf16[768,2304]{1,0:T(8,128)(2,1)} %refs_2_.5, ...), custom_call_target="tpu_custom_call" | custom-call | tf_op jit(solution)/shard_map/pair_core/pallas_call | solution.py:273
  74.7 20.1 %pair_core.4 = (f32[16,128]{1,0:T(8,128)}, bf16[256,768]{1,0:T(8,128)(2,1)}, bf16[256,768]{1,0:T(8,128)(2,1)}, bf16[256,768]{1,0:T(8,128)(2,1)}, bf16[256,2304]{...) custom-call(s32[16]{0:T(128)} %refs_0_.5, bf16[512,768]{1,0:T(8,128)(2,1)} %bitcast.128, ...), custom_call_target="tpu_custom_call" | custom-call | tf_op jit(solution)/shard_map/pair_core/pallas_call | solution.py:273
  94.8 20.1 %pair_core.5 = (f32[16,128]{1,0:T(8,128)}, bf16[256,768]{1,0:T(8,128)(2,1)}, bf16[256,768]{1,0:T(8,128)(2,1)}, bf16[256,768]{1,0:T(8,128)(2,1)}, bf16[256,2304]{...) custom-call(s32[16]{0:T(128)} %refs_0_.5, bf16[512,768]{1,0:T(8,128)(2,1)} %bitcast.13.refs_1_, ...), custom_call_target="tpu_custom_call" | custom-call | tf_op jit(solution)/shard_map/pair_core/pallas_call | solution.py:273
  114.9 6.8 %weight_gradients.4 = bf16[384,2304]{1,0:T(8,128)(2,1)} custom-call(s32[1]{0:T(128)} %bitcast.26.core.at, bf16[256,768]{1,0:T(8,128)(2,1)} %bitcast.122, bf16[256,768]{1,0:T(8,128)(2,1)} %get-tuple-element.46.refs_1_, bf16[256,768]{1,0:T(8,128)(2,1)} %get-tuple-element.47.refs_2_, bf16[256,2304]{1,0:T(8,128)(2,1)} %get-tuple-element.48.refs_3_, ...), custom_call_target="tpu_custom_call" | custom-call | tf_op jit(solution)/shard_map/weight_gradients/pallas_call | solution.py:480
  121.9 5.0 %weight_gradients.5 = (bf16[384,768]{1,0:T(8,128)(2,1)}, bf16[384,768]{1,0:T(8,128)(2,1)}) custom-call(s32[1]{0:T(128)} %bitcast.26.core.at, bf16[256,768]{1,0:T(8,128)(2,1)} %get-tuple-element.51.refs_0_, bf16[256,768]{1,0:T(8,128)(2,1)} %get-tuple-element.52.refs_1_, bf16[256,768]{1,0:T(8,128)(2,1)} %get-tuple-element.53.refs_2_, ...), custom_call_target="tpu_custom_call" | custom-call | tf_op jit(solution)/shard_map/weight_gradients/pallas_call | solution.py:480
  127.2 6.8 %weight_gradients.3 = bf16[384,2304]{1,0:T(8,128)(2,1)} custom-call(s32[1]{0:T(128)} %bitcast.26.core.at, bf16[256,768]{1,0:T(8,128)(2,1)} %bitcast.123, bf16[256,768]{1,0:T(8,128)(2,1)} %get-tuple-element.46.refs_1_, bf16[256,768]{1,0:T(8,128)(2,1)} %get-tuple-element.47.refs_2_, bf16[256,2304]{1,0:T(8,128)(2,1)} %get-tuple-element.48.refs_3_, ...), custom_call_target="tpu_custom_call" | custom-call | tf_op jit(solution)/shard_map/weight_gradients/pallas_call | solution.py:480
  134.0 5.9 %all-to-all-start.3 = ((bf16[32,1,16,768]{3,2,1,0:T(8,128)(2,1)}), bf16[32,1,16,768]{3,2,1,0:T(8,128)(2,1)}, u32[]{:S(2)}, u32[]{:S(2)}) async-start(bf16[32,1,16,768]{3,2,1,0:T(8,128)(2,1)} %bitcast.144), calls=%async_computation.3 | async-start | bytes 1572864 | tf_op jit(solution)/shard_map/all_to_all | solution.py:604
  149.5 11.3 %collective-permute-done.14 = bf16[96,768]{1,0:T(8,128)(2,1)S(1)} collective-permute-done((bf16[96,768]{1,0:T(8,128)(2,1)S(1)}, bf16[96,768]{1,0:T(8,128)(2,1)S(1)}, u32[]{:S(2)}, u32[]{:S(2)}) %collective-permute-start.14) | collective-permute-done | bytes 147488 | tf_op jit(solution)/shard_map/ppermute | solution.py:546
  160.8 12.2 %collective-permute-done.15 = bf16[96,768]{1,0:T(8,128)(2,1)S(1)} collective-permute-done((bf16[96,768]{1,0:T(8,128)(2,1)S(1)}, bf16[96,768]{1,0:T(8,128)(2,1)S(1)}, u32[]{:S(2)}, u32[]{:S(2)}) %collective-permute-start.15) | collective-permute-done | bytes 147488 | tf_op jit(solution)/shard_map/ppermute | solution.py:546
  176.5 6.7 %collective-permute-done.2 = bf16[96,2304]{1,0:T(8,128)(2,1)S(1)} collective-permute-done((bf16[96,2304]{1,0:T(8,128)(2,1)S(1)}, bf16[96,2304]{1,0:T(8,128)(2,1)S(1)}, u32[]{:S(2)}, u32[]{:S(2)}) %collective-permute-start.2) | collective-permute-done | bytes 442400 | tf_op jit(solution)/shard_map/ppermute | solution.py:546
  183.5 3.8 %collective-permute-start.5 = (bf16[24,2304]{1,0:T(8,128)(2,1)S(1)}, bf16[24,2304]{1,0:T(8,128)(2,1)S(1)}, u32[]{:S(2)}, u32[]{:S(2)}) collective-permute-start(bf16[24,2304]{1,0:T(8,128)(2,1)S(1)} %get-tuple-element.62), channel_id=1, source_target_pairs={{0,24},{1,25},{2,26},{3,27},{4,28},{5,29},{6,30},{7,31},{8,0},{9,1... | collective-permute-start | bytes 331784 | tf_op jit(solution)/shard_map/ppermute | solution.py:546
  188.9 2.4 collective-permute-done.3
  191.3 3.9 %collective-permute-done.4 = bf16[24,2304]{1,0:T(8,128)(2,1)S(1)} collective-permute-done((bf16[24,2304]{1,0:T(8,128)(2,1)S(1)}, bf16[24,2304]{1,0:T(8,128)(2,1)S(1)}, u32[]{:S(2)}, u32[]{:S(2)}) %collective-permute-start.4) | collective-permute-done | bytes 110624 | tf_op jit(solution)/shard_map/ppermute | solution.py:546
  196.2 2.4 collective-permute-start.7
  200.0 3.2 %collective-permute-done.6 = bf16[24,2304]{1,0:T(8,128)(2,1)S(1)} collective-permute-done((bf16[24,2304]{1,0:T(8,128)(2,1)S(1)}, bf16[24,2304]{1,0:T(8,128)(2,1)S(1)}, u32[]{:S(2)}, u32[]{:S(2)}) %collective-permute-start.6) | collective-permute-done | bytes 110624 | tf_op jit(solution)/shard_map/ppermute | solution.py:546
  203.2 3.6 %collective-permute-done.7 = bf16[24,2304]{1,0:T(8,128)(2,1)S(1)} collective-permute-done((bf16[24,2304]{1,0:T(8,128)(2,1)S(1)}, bf16[24,2304]{1,0:T(8,128)(2,1)S(1)}, u32[]{:S(2)}, u32[]{:S(2)}) %collective-permute-start.7) | collective-permute-done | bytes 110624 | tf_op jit(solution)/shard_map/ppermute | solution.py:546
  209.1 3.8 %collective-permute-done.20 = bf16[48,768]{1,0:T(8,128)(2,1)S(1)} collective-permute-done((bf16[48,768]{1,0:T(8,128)(2,1)S(1)}, bf16[48,768]{1,0:T(8,128)(2,1)S(1)}, u32[]{:S(2)}, u32[]{:S(2)}) %collective-permute-start.20) | collective-permute-done | bytes 73760 | tf_op jit(solution)/shard_map/ppermute | solution.py:546
  212.9 2.4 collective-permute-done.9
  217.7 2.5 collective-permute-start.21
  220.2 3.4 %all-to-all-start.4 = ((bf16[32,1,16,768]{3,2,1,0:T(8,128)(2,1)}), bf16[32,1,16,768]{3,2,1,0:T(8,128)(2,1)}, u32[]{:S(2)}, u32[]{:S(2)}) async-start(bf16[32,1,16,768]{3,2,1,0:T(8,128)(2,1)} %bitcast.143), calls=%async_computation.4 | async-start | bytes 1572864 | tf_op jit(solution)/shard_map/all_to_all | solution.py:604
  224.7 2.6 collective-permute-start.22
  232.7 18.1 %collective-permute-done.22 = bf16[96,768]{1,0:T(8,128)(2,1)S(1)} collective-permute-done((bf16[96,768]{1,0:T(8,128)(2,1)}, bf16[96,768]{1,0:T(8,128)(2,1)S(1)}, u32[]{:S(2)}, u32[]{:S(2)}) %collective-permute-start.22) | collective-permute-done | bytes 147488 | tf_op jit(solution)/shard_map/ppermute | solution.py:546
  255.5 2.7 fusion.3
  260.2 3.5 %receive.1 = bf16[256,768]{1,0:T(8,128)(2,1)} custom-call(s32[32,2]{1,0:T(8,128)} %copy.34.wanted, f32[256,768]{1,0:T(8,128)} %get-tuple-element.43.own, bf16[512,768]{1,0:T(8,128)(2,1)} %bitcast.20.first, bf16[512,768]{1,0:T(8,128)(2,1)} %bitcast.23.second), custom_call_target="tpu_custom_call" | custom-call | tf_op jit(solution)/shard_map/receive/pallas_call | solution.py:339
  265.8 2.3 finish.6.refs_0_
  268.1 2.3 finish.7.refs_0_
  272.6 2.3 finish.9
  (113 shorter events, 47.5 us)
Async XLA Ops:
  20.6 30.0 %copy-start.7 = (f32[768]{0:T(1024)S(1)}, f32[768]{0:T(1024)}, u32[]{:S(2)}) copy-start(f32[768]{0:T(1024)} %param.18) | copy-start | bytes 9220
  20.6 30.6 %copy-start.8 = (f32[768]{0:T(1024)S(1)}, f32[768]{0:T(1024)}, u32[]{:S(2)}) copy-start(f32[768]{0:T(1024)} %param.19) | copy-start | bytes 9220
  20.6 31.2 %copy-start = (bf16[768,2304]{1,0:T(8,128)(2,1)S(1)}, bf16[768,2304]{1,0:T(8,128)(2,1)}, u32[]{:S(2)}) copy-start(bf16[768,2304]{1,0:T(8,128)(2,1)} %refs_2_.5) | copy-start | bytes 10616836
  46.9 47.8 %all-to-all-start.2 = ((bf16[32,1,16,768]{3,2,1,0:T(8,128)(2,1)}), bf16[32,1,16,768]{3,2,1,0:T(8,128)(2,1)}, u32[]{:S(2)}, u32[]{:S(2)}) async-start(bf16[32,1,16,768]{3,2,1,0:T(8,128)(2,1)} %bitcast.145), calls=%async_computation.2 | async-start | bytes 1572864 | tf_op jit(solution)/shard_map/all_to_all | solution.py:604
  121.7 26.1 %collective-permute-start = (bf16[384,2304]{1,0:T(8,128)(2,1)}, bf16[384,2304]{1,0:T(8,128)(2,1)S(1)}, u32[]{:S(2)}, u32[]{:S(2)}) collective-permute-start(bf16[384,2304]{1,0:T(8,128)(2,1)} %weight_gradients.4), channel_id=1, source_target_pairs={{0,1},{1,0},{2,3},{3,2},{4,5},{5,4},{6,7},{7,6},{8,9},{9,8},{10,11... | collective-permute-start | bytes 5308424 | tf_op jit(solution)/shard_map/ppermute | solution.py:546
  126.8 14.1 %collective-permute-start.13 = (bf16[384,768]{1,0:T(8,128)(2,1)}, bf16[384,768]{1,0:T(8,128)(2,1)}, u32[]{:S(2)}, u32[]{:S(2)}) collective-permute-start(bf16[384,768]{1,0:T(8,128)(2,1)} %get-tuple-element.58), channel_id=1, source_target_pairs={{0,1},{1,0},{2,3},{3,2},{4,5},{5,4},{6,7},{7,6},{8,9},{9,8},{10,11... | collective-permute-start | bytes 1769480 | tf_op jit(solution)/shard_map/ppermute | solution.py:546
  134.0 86.2 %all-to-all-start.3 = ((bf16[32,1,16,768]{3,2,1,0:T(8,128)(2,1)}), bf16[32,1,16,768]{3,2,1,0:T(8,128)(2,1)}, u32[]{:S(2)}, u32[]{:S(2)}) async-start(bf16[32,1,16,768]{3,2,1,0:T(8,128)(2,1)} %bitcast.144), calls=%async_computation.3 | async-start | bytes 1572864 | tf_op jit(solution)/shard_map/all_to_all | solution.py:604
  142.1 18.6 %collective-permute-start.14 = (bf16[96,768]{1,0:T(8,128)(2,1)S(1)}, bf16[96,768]{1,0:T(8,128)(2,1)S(1)}, u32[]{:S(2)}, u32[]{:S(2)}) collective-permute-start(bf16[96,768]{1,0:T(8,128)(2,1)S(1)} %get-tuple-element.64), channel_id=1, source_target_pairs={{0,8},{1,9},{2,10},{3,11},{4,12},{5,13},{6,14},{7,15},{8,16},{9,17... | collective-permute-start | bytes 442376 | tf_op jit(solution)/shard_map/ppermute | solution.py:546
  143.9 16.9 %collective-permute-start.16 = (bf16[96,768]{1,0:T(8,128)(2,1)S(1)}, bf16[96,768]{1,0:T(8,128)(2,1)S(1)}, u32[]{:S(2)}, u32[]{:S(2)}) collective-permute-start(bf16[96,768]{1,0:T(8,128)(2,1)S(1)} %get-tuple-element.65), channel_id=1, source_target_pairs={{0,24},{1,25},{2,26},{3,27},{4,28},{5,29},{6,30},{7,31},{8,0},{9,1... | collective-permute-start | bytes 442376 | tf_op jit(solution)/shard_map/ppermute | solution.py:546
  146.0 26.9 %collective-permute-start.15 = (bf16[96,768]{1,0:T(8,128)(2,1)S(1)}, bf16[96,768]{1,0:T(8,128)(2,1)S(1)}, u32[]{:S(2)}, u32[]{:S(2)}) collective-permute-start(bf16[96,768]{1,0:T(8,128)(2,1)S(1)} %get-tuple-element.66), channel_id=1, source_target_pairs={{0,16},{1,17},{2,18},{3,19},{4,20},{5,21},{6,22},{7,23},{8,24},{9,... | collective-permute-start | bytes 442376 | tf_op jit(solution)/shard_map/ppermute | solution.py:546
  148.0 26.7 %collective-permute-start.1 = (bf16[192,2304]{1,0:T(8,128)(2,1)S(1)}, bf16[192,2304]{1,0:T(8,128)(2,1)S(1)}, u32[]{:S(2)}, u32[]{:S(2)}) collective-permute-start(bf16[192,2304]{1,0:T(8,128)(2,1)S(1)} %fusion.6), channel_id=1, source_target_pairs={{0,2},{1,5},{2,0},{3,7},{4,6},{5,1},{6,4},{7,3},{8,10},{9,13},{10,... | collective-permute-start | bytes 2654216 | tf_op jit(solution)/shard_map/ppermute | solution.py:546
  173.0 14.3 %collective-permute-start.17 = (bf16[48,768]{1,0:T(8,128)(2,1)S(1)}, bf16[48,768]{1,0:T(8,128)(2,1)S(1)}, u32[]{:S(2)}, u32[]{:S(2)}) collective-permute-start(bf16[48,768]{1,0:T(8,128)(2,1)S(1)} %fusion.17), channel_id=1, source_target_pairs={{0,2},{1,5},{2,0},{3,7},{4,6},{5,1},{6,4},{7,3},{8,10},{9,13},{10,... | collective-permute-start | bytes 221192 | tf_op jit(solution)/shard_map/ppermute | solution.py:546
  174.8 8.4 %collective-permute-start.2 = (bf16[96,2304]{1,0:T(8,128)(2,1)S(1)}, bf16[96,2304]{1,0:T(8,128)(2,1)S(1)}, u32[]{:S(2)}, u32[]{:S(2)}) collective-permute-start(bf16[96,2304]{1,0:T(8,128)(2,1)S(1)} %fusion.7), channel_id=1, source_target_pairs={{0,4},{1,3},{2,6},{3,1},{4,0},{5,7},{6,2},{7,5},{8,12},{9,11},{10,... | collective-permute-start | bytes 1327112 | tf_op jit(solution)/shard_map/ppermute | solution.py:546
  183.4 7.9 %collective-permute-start.3 = (bf16[24,2304]{1,0:T(8,128)(2,1)S(1)}, bf16[24,2304]{1,0:T(8,128)(2,1)S(1)}, u32[]{:S(2)}, u32[]{:S(2)}) collective-permute-start(bf16[24,2304]{1,0:T(8,128)(2,1)S(1)} %get-tuple-element.61), channel_id=1, source_target_pairs={{0,8},{1,9},{2,10},{3,11},{4,12},{5,13},{6,14},{7,15},{8,16},{9,17... | collective-permute-start | bytes 331784 | tf_op jit(solution)/shard_map/ppermute | solution.py:546
  183.5 7.8 %collective-permute-start.5 = (bf16[24,2304]{1,0:T(8,128)(2,1)S(1)}, bf16[24,2304]{1,0:T(8,128)(2,1)S(1)}, u32[]{:S(2)}, u32[]{:S(2)}) collective-permute-start(bf16[24,2304]{1,0:T(8,128)(2,1)S(1)} %get-tuple-element.62), channel_id=1, source_target_pairs={{0,24},{1,25},{2,26},{3,27},{4,28},{5,29},{6,30},{7,31},{8,0},{9,1... | collective-permute-start | bytes 331784 | tf_op jit(solution)/shard_map/ppermute | solution.py:546
  187.3 7.9 %collective-permute-start.4 = (bf16[24,2304]{1,0:T(8,128)(2,1)S(1)}, bf16[24,2304]{1,0:T(8,128)(2,1)S(1)}, u32[]{:S(2)}, u32[]{:S(2)}) collective-permute-start(bf16[24,2304]{1,0:T(8,128)(2,1)S(1)} %get-tuple-element.63), channel_id=1, source_target_pairs={{0,16},{1,17},{2,18},{3,19},{4,20},{5,21},{6,22},{7,23},{8,24},{9,... | collective-permute-start | bytes 331784 | tf_op jit(solution)/shard_map/ppermute | solution.py:546
  187.3 8.1 %collective-permute-start.18 = (bf16[24,768]{1,0:T(8,128)(2,1)S(1)}, bf16[24,768]{1,0:T(8,128)(2,1)S(1)}, u32[]{:S(2)}, u32[]{:S(2)}) collective-permute-start(bf16[24,768]{1,0:T(8,128)(2,1)S(1)} %fusion.19), channel_id=1, source_target_pairs={{0,4},{1,3},{2,6},{3,1},{4,0},{5,7},{6,2},{7,5},{8,12},{9,11},{10,... | collective-permute-start | bytes 110600 | tf_op jit(solution)/shard_map/ppermute | solution.py:546
  195.3 7.8 %collective-permute-start.6 = (bf16[24,2304]{1,0:T(8,128)(2,1)S(1)}, bf16[24,2304]{1,0:T(8,128)(2,1)S(1)}, u32[]{:S(2)}, u32[]{:S(2)}) collective-permute-start(bf16[24,2304]{1,0:T(8,128)(2,1)S(1)} %get-tuple-element.60), channel_id=1, source_target_pairs={{0,8},{1,9},{2,10},{3,11},{4,12},{5,13},{6,14},{7,15},{8,16},{9,17... | collective-permute-start | bytes 331784 | tf_op jit(solution)/shard_map/ppermute | solution.py:546
  195.5 12.1 %collective-permute-start.19 = (bf16[24,768]{1,0:T(8,128)(2,1)S(1)}, bf16[24,768]{1,0:T(8,128)(2,1)S(1)}, u32[]{:S(2)}, u32[]{:S(2)}) collective-permute-start(bf16[24,768]{1,0:T(8,128)(2,1)S(1)} %fusion.18), channel_id=1, source_target_pairs={{0,4},{1,3},{2,6},{3,1},{4,0},{5,7},{6,2},{7,5},{8,12},{9,11},{10,... | collective-permute-start | bytes 110600 | tf_op jit(solution)/shard_map/ppermute | solution.py:546
  196.2 10.6 %collective-permute-start.7 = (bf16[24,2304]{1,0:T(8,128)(2,1)S(1)}, bf16[24,2304]{1,0:T(8,128)(2,1)S(1)}, u32[]{:S(2)}, u32[]{:S(2)}) collective-permute-start(bf16[24,2304]{1,0:T(8,128)(2,1)S(1)} %get-tuple-element.60), channel_id=1, source_target_pairs={{0,16},{1,17},{2,18},{3,19},{4,20},{5,21},{6,22},{7,23},{8,24},{9,... | collective-permute-start | bytes 331784 | tf_op jit(solution)/shard_map/ppermute | solution.py:546
  198.6 8.2 %collective-permute-start.8 = (bf16[24,2304]{1,0:T(8,128)(2,1)S(1)}, bf16[24,2304]{1,0:T(8,128)(2,1)S(1)}, u32[]{:S(2)}, u32[]{:S(2)}) collective-permute-start(bf16[24,2304]{1,0:T(8,128)(2,1)S(1)} %get-tuple-element.60), channel_id=1, source_target_pairs={{0,24},{1,25},{2,26},{3,27},{4,28},{5,29},{6,30},{7,31},{8,0},{9,1... | collective-permute-start | bytes 331784 | tf_op jit(solution)/shard_map/ppermute | solution.py:546
  206.9 8.4 %collective-permute-start.9 = (bf16[96,2304]{1,0:T(8,128)(2,1)S(1)}, bf16[96,2304]{1,0:T(8,128)(2,1)S(1)}, u32[]{:S(2)}, u32[]{:S(2)}) collective-permute-start(bf16[96,2304]{1,0:T(8,128)(2,1)S(1)} %bitcast.137), channel_id=1, source_target_pairs={{0,4},{1,3},{2,6},{3,1},{4,0},{5,7},{6,2},{7,5},{8,12},{9,11},{10,... | collective-permute-start | bytes 1327112 | tf_op jit(solution)/shard_map/ppermute | solution.py:546
  207.6 5.2 %collective-permute-start.20 = (bf16[48,768]{1,0:T(8,128)(2,1)S(1)}, bf16[48,768]{1,0:T(8,128)(2,1)S(1)}, u32[]{:S(2)}, u32[]{:S(2)}) collective-permute-start(bf16[48,768]{1,0:T(8,128)(2,1)S(1)} %pad_maximum_fusion.2), channel_id=1, source_target_pairs={{0,2},{1,5},{2,0},{3,7},{4,6},{5,1},{6,4},{7,3},{8,10},{9,13},{10,... | collective-permute-start | bytes 221192 | tf_op jit(solution)/shard_map/ppermute | solution.py:546
  216.4 35.2 %collective-permute-start.10 = (bf16[192,2304]{1,0:T(8,128)(2,1)}, bf16[192,2304]{1,0:T(8,128)(2,1)}, u32[]{:S(2)}, u32[]{:S(2)}) collective-permute-start(bf16[192,2304]{1,0:T(8,128)(2,1)} %pad_maximum_fusion.part), channel_id=1, source_target_pairs={{0,2},{1,5},{2,0},{3,7},{4,6},{5,1},{6,4},{7,3},{8,10},{9,13},{10,... | collective-permute-start | bytes 2654216 | tf_op jit(solution)/shard_map/ppermute | solution.py:546
  217.0 38.5 %copy-start.1 = (bf16[768,2304]{1,0:T(8,128)(2,1)S(1)}, bf16[768,2304]{1,0:T(8,128)(2,1)}, u32[]{:S(2)}) copy-start(bf16[768,2304]{1,0:T(8,128)(2,1)} %refs_2_.5) | copy-start | bytes 10616836
  217.7 13.4 %collective-permute-start.21 = (bf16[96,768]{1,0:T(8,128)(2,1)}, bf16[96,768]{1,0:T(8,128)(2,1)}, u32[]{:S(2)}, u32[]{:S(2)}) collective-permute-start(bf16[96,768]{1,0:T(8,128)(2,1)} %pad_maximum_fusion.1), channel_id=1, source_target_pairs={{0,8},{1,9},{2,10},{3,11},{4,12},{5,13},{6,14},{7,15},{8,16},{9,17... | collective-permute-start | bytes 442376 | tf_op jit(solution)/shard_map/ppermute | solution.py:546
  220.2 40.1 %all-to-all-start.4 = ((bf16[32,1,16,768]{3,2,1,0:T(8,128)(2,1)}), bf16[32,1,16,768]{3,2,1,0:T(8,128)(2,1)}, u32[]{:S(2)}, u32[]{:S(2)}) async-start(bf16[32,1,16,768]{3,2,1,0:T(8,128)(2,1)} %bitcast.143), calls=%async_computation.4 | async-start | bytes 1572864 | tf_op jit(solution)/shard_map/all_to_all | solution.py:604
  224.7 26.1 %collective-permute-start.22 = (bf16[96,768]{1,0:T(8,128)(2,1)}, bf16[96,768]{1,0:T(8,128)(2,1)S(1)}, u32[]{:S(2)}, u32[]{:S(2)}) collective-permute-start(bf16[96,768]{1,0:T(8,128)(2,1)} %pad_maximum_fusion.1), channel_id=1, source_target_pairs={{0,16},{1,17},{2,18},{3,19},{4,20},{5,21},{6,22},{7,23},{8,24},{9,... | collective-permute-start | bytes 442376 | tf_op jit(solution)/shard_map/ppermute | solution.py:546
  227.3 24.7 %collective-permute-start.23 = (bf16[96,768]{1,0:T(8,128)(2,1)}, bf16[96,768]{1,0:T(8,128)(2,1)S(1)}, u32[]{:S(2)}, u32[]{:S(2)}) collective-permute-start(bf16[96,768]{1,0:T(8,128)(2,1)} %pad_maximum_fusion.1), channel_id=1, source_target_pairs={{0,24},{1,25},{2,26},{3,27},{4,28},{5,29},{6,30},{7,31},{8,0},{9,1... | collective-permute-start | bytes 442376 | tf_op jit(solution)/shard_map/ppermute | solution.py:546
  251.5 16.5 %collective-permute-start.12 = (bf16[192,2304]{1,0:T(8,128)(2,1)}, bf16[192,2304]{1,0:T(8,128)(2,1)}, u32[]{:S(2)}, u32[]{:S(2)}) collective-permute-start(bf16[192,2304]{1,0:T(8,128)(2,1)} %pad_maximum_fusion.part), channel_id=1, source_target_pairs={{0,1},{1,0},{2,3},{3,2},{4,5},{5,4},{6,7},{7,6},{8,9},{9,8},{10,11... | collective-permute-start | bytes 2654216 | tf_op jit(solution)/shard_map/ppermute | solution.py:546
  251.5 21.1 %collective-permute-start.11 = (bf16[192,2304]{1,0:T(8,128)(2,1)}, bf16[192,2304]{1,0:T(8,128)(2,1)}, u32[]{:S(2)}, u32[]{:S(2)}) collective-permute-start(bf16[192,2304]{1,0:T(8,128)(2,1)} %collective-permute-done.10.part), channel_id=1, source_target_pairs={{0,1},{1,0},{2,3},{3,2},{4,5},{5,4},{6,7},{7,6},{8,9},{9,8},{10,11... | collective-permute-start | bytes 2654216 | tf_op jit(solution)/shard_map/ppermute | solution.py:546
  252.7 11.0 %collective-permute-start.24 = (bf16[384,768]{1,0:T(8,128)(2,1)}, bf16[384,768]{1,0:T(8,128)(2,1)}, u32[]{:S(2)}, u32[]{:S(2)}) collective-permute-start(bf16[384,768]{1,0:T(8,128)(2,1)} %bitcast.74.part), channel_id=1, source_target_pairs={{0,1},{1,0},{2,3},{3,2},{4,5},{5,4},{6,7},{7,6},{8,9},{9,8},{10,11... | collective-permute-start | bytes 1769480 | tf_op jit(solution)/shard_map/ppermute | solution.py:546
  (8 other events, 81.0 us)
where the time goes:
time: 276 us; the launch traced here: 275 us
  Pallas kernels  99.5 us (36%)
  waiting for transfers between devices  67.5 us (24%)
  starting transfers between devices  42.5 us (15%)
  blocking collectives  38.3 us (14%)
  local copies, waits for them, and re-layouts  12.7 us (5%)
  other arithmetic  7.96 us (3%)
  matrix products  5.39 us (2%)
    ppermute x25, waiting for transfers between devices, shifted(): return lax.ppermute(x, 'dp', table)  67.5 us
    pallas_call x3, Pallas kernels, pair_core(): pl.pallas_call(body, out_shape=out, in_specs=specs, out_specs=[vm] + [far...  59.8 us
    ppermute x25, starting transfers between devices, shifted(): return lax.ppermute(x, 'dp', table)  29.7 us
    all_to_all x1, blocking collectives, exchange(): moved = lax.all_to_all(split, 'dp', split_axis=0, concat_axis=0, tiled=True)  23.9 us
    pallas_call x3, Pallas kernels, weight_gradients(): pl.pallas_call(functools.partial(weight_kernel, flips=flips, groups=group...  18.6 us
    all_to_all x1, blocking collectives, step(): lax.all_to_all(wanted, 'dp', split_axis=0, concat_axis=0, tiled=True)  14.4 us
    pallas_call x6, Pallas kernels, finish(): pl.pallas_call(functools.partial(finish_kernel, factor=factor), grid_spec...  13.1 us
    all_to_all x3, starting transfers between devices, exchange(): moved = lax.all_to_all(split, 'dp', split_axis=0, concat_axis=0, tiled=True)  12.9 us
  transfers between devices with their start and end apart: 28, of which 10 were waited for; matrix products, arithmetic and copies ran while one was open for 8% of the time, Pallas kernels for 24%

commit v1 on v0

--- a/solution.py
+++ b/solution.py
@@ -31,8 +31,8 @@
     loads.append(pltpu.make_async_copy(wo_h, wo, sem_in.at[3]))
     if not positive:
         loads.append(pltpu.make_async_copy(text_h, text_in, sem_in.at[4]))
-    for load in loads:
-        load.start()
+    loads[0].start()
+    loads[1].start()
     saves = []
 
     def save(src, dst):
@@ -134,8 +134,10 @@
     per = width // 256
     for n in range(3):
         loads[n].wait()
-        lax.fori_loop(n * per, (n + 1) * per, project, 0)
-    lax.fori_loop(0, pairs_of_units, forward, 0)
+        for load in loads[2:3] if n == 0 else loads[3:] if n == 1 else []:
+            load.start()
+        lax.fori_loop(n * per, (n + 1) * per, project, 0, unroll=3)
+    lax.fori_loop(0, pairs_of_units, forward, 0, unroll=4)
     save(ctx, ctx_h)
     loads[3].wait()
 
@@ -175,7 +177,7 @@
         dctx[rs, :] = dot_nt(gl, wo[...]).astype(BF)
         return carry
 
-    lax.fori_loop(0, rows // chunk, middle, 0)
+    lax.fori_loop(0, rows // chunk, middle, 0, unroll=2)
     save(ga, ga_h)
     if not positive:
         loads[4].wait()
@@ -214,7 +216,7 @@
             copy.start()
         return carry
 
-    lax.fori_loop(0, pairs_of_units, backward, 0)
+    lax.fori_loop(0, pairs_of_units, backward, 0, unroll=2)
 
     def images(n, carry):
         cols = pl.ds(pl.multiple_of(n * 256, 256), 256)
@@ -225,7 +227,7 @@
             gh[:, cols] = g
         return carry
 
-    lax.fori_loop(0, width // 256, images, 0)
+    lax.fori_loop(0, width // 256, images, 0, unroll=3)
     if not positive:
         back[...] = jnp.zeros(back.shape, BF)
         for i in range(rows // 16):
@@ -343,14 +345,15 @@
         out_specs=vm,
         scratch_shapes=[pltpu.VMEM(own.shape, F32)],
         name="receive",
+        compiler_params=pltpu.CompilerParams(vmem_limit_bytes=56 * 1024 * 1024),
     )(wanted, own, first, second)
 
 
-def route_kernel(owner, slot, wanted, owners, color0):
-    count = owner.shape[0]
+def route_kernel(named, wanted, owners, color0):
+    count = named.shape[0]
     n = 2 * count
     peers = wanted.shape[0]
-    o0, o1 = owner[:, 0:1], owner[:, 1:2]
+    o0, o1 = named[:, 0:1], named[:, 1:2]
     i = lax.broadcasted_iota(jnp.int32, (n, n), 0)
     k = lax.broadcasted_iota(jnp.int32, (n, n), 1)
     i_swap = jnp.where(i < count, i + count, i - count)
@@ -363,7 +366,7 @@
     swap_col = jnp.concatenate([o1, o0], axis=0)
     owner_row = row_of(owner_col)
     swap_row = row_of(swap_col)
-    slot_row = row_of(jnp.concatenate([slot[:, 0:1], slot[:, 1:2]], axis=0))
+    slot_row = row_of(jnp.concatenate([named[:, 2:3], named[:, 3:4]], axis=0))
     ahead = (owner_col == swap_row) & (i != k_swap)
     behind = (owner_row == swap_col) & (k != i_swap)
     reach = jnp.where(ahead | behind | (i == k), 1.0, 0.0)
@@ -402,13 +405,14 @@
             jax.ShapeDtypeStruct((2, count), jnp.int32),
             jax.ShapeDtypeStruct((1, count), jnp.int32),
         ],
-        in_specs=[vm, vm],
+        in_specs=[vm],
         out_specs=[vm, vm, vm],
         name="route",
-    )(owner, slot)
-
-
-def weight_kernel(core, *refs, flips, groups, with_text):
+    )(jnp.concatenate([owner, slot], axis=1))
+
+
+def weight_kernel(core, *refs, size, groups, with_text):
+    flips = (1, 0)
     xs = refs[:groups]
     ds = refs[groups : 2 * groups]
     rest = refs[2 * groups :]
@@ -424,6 +428,7 @@
     rows_of, width = xs[0].shape
     half = width // 2
     per = width // 256
+    block_rows = half // size
     for flip, out, hold in zip(flips, outs, turned):
         for part in range(2):
 
@@ -443,7 +448,11 @@
                 acc = acc + dot_nn(hold[:, g * rows_of : (g + 1) * rows_of], ds[g][:, cols])
             if more:
                 acc = acc + dot_nn(hold[:, groups * rows_of :], dt[:, cols])
-            out[:, cols] = acc.astype(BF)
+            low = acc.astype(BF)
+            for p in range(size):
+                to = ((p + size - core[1 + flip]) % size) * block_rows
+                rows = pl.ds(pl.multiple_of(to, block_rows), block_rows)
+                out[rows, cols] = low[p * block_rows : (p + 1) * block_rows]
             return carry
 
         if with_text:
@@ -460,7 +469,8 @@
             lax.fori_loop(0, per, functools.partial(columns, more=False), 0)
 
 
-def weight_gradients(core, flips, xs, ds, text, dt):
+def weight_gradients(core, size, xs, ds, text, dt):
+    flips = (1, 0)
     groups = len(xs)
     with_text = text is not None
     rows_of, width = xs[0].shape
@@ -478,7 +488,7 @@
         depth += text.shape[0]
     half = width // 2
     return pl.pallas_call(
-        functools.partial(weight_kernel, flips=flips, groups=groups, with_text=with_text),
+        functools.partial(weight_kernel, size=size, groups=groups, with_text=with_text),
         grid_spec=pltpu.PrefetchScalarGridSpec(
             num_scalar_prefetch=1,
             grid=(ds[0].shape[1] // width,),
@@ -492,28 +502,39 @@
     )(core, *arrays)
 
 
-def finish_kernel(at, part, *refs, factor):
-    refs[-1][...] = part[...].astype(F32) * factor
-
-
-def finish(at, part, rows, factor, before):
-    count, total = part.shape
-    steps = 2 if count % 32 == 0 else 1
-    block = count // steps
+def finish_kernel(at, *refs, count, factor):
+    for p in range(count):
+
+        @pl.when(pl.program_id(0) == p)
+        def _():
+            refs[-1][...] = refs[p][...].astype(F32) * factor
+
+
+def finish(places, parts, rows, factor, before):
+    n = len(parts)
+    height, total = parts[0].shape
+    steps = 2 if height % 32 == 0 else 1
+    block = height // steps
     given = [] if before is None else [before]
+
+    def source(p):
+        last = steps - 1
+        return lambda g, i, at: (jnp.where(g == p, i, jnp.where(g > p, last, 0)), 0)
+
     return pl.pallas_call(
-        functools.partial(finish_kernel, factor=factor),
+        functools.partial(finish_kernel, count=n, factor=factor),
         grid_spec=pltpu.PrefetchScalarGridSpec(
             num_scalar_prefetch=1,
-            grid=(steps,),
-            in_specs=[pl.BlockSpec((block, total), lambda i, at: (i, 0))]
+            grid=(n, steps),
+            in_specs=[pl.BlockSpec((block, total), source(p)) for p in range(n)]
             + [pl.BlockSpec(memory_space=pl.ANY)] * len(given),
-            out_specs=pl.BlockSpec((block, total), lambda i, at: (at[0] * steps + i, 0)),
+            out_specs=pl.BlockSpec((block, total), lambda g, i, at: (at[g] * steps + i, 0)),
         ),
         out_shape=jax.ShapeDtypeStruct((rows, total), F32),
-        input_output_aliases={2: 0} if given else {},
+        input_output_aliases={1 + n: 0} if given else {},
         name="finish",
-    )(at.reshape(1), part, *given)
+        compiler_params=pltpu.CompilerParams(vmem_limit_bytes=60 * 1024 * 1024),
+    )(places[0].reshape(1) if n == 1 else jnp.stack(places), *parts, *given)
 
 
 def grid_of(mesh):
@@ -551,6 +572,15 @@
     for t in terms[1:]:
         total = total + t.astype(F32)
     return total
+
+
+def scatter_ready(terms, dims):
+    size = dims[0][1]
+    split = [t.reshape((size, t.shape[0] // size) + t.shape[1:]) for t in terms]
+    got = [
+        shifted(total_of([t[k] for t in split]).astype(BF), dims, k) for k in range(1, size)
+    ]
+    return [t[0] for t in split] + got
 
 
 def scatter_terms(terms, dims):
@@ -644,15 +674,24 @@
     deep = (z_dim, z_dim)
     factor = 1.0 / (captions * peers)
 
-    keep_a, send_a = weight_gradients(
-        core, (0, 1), [r[3] for r in results], [r[2] for r in results], None, None
+    size = flat_first[0][1]
+    at = by_core(*flat_first)
+    other_at = by_core(flat_first[1], flat_first[0])
+    deep_at = coord(z_dim)
+    send_a, keep_a = weight_gradients(
+        jnp.stack([core[0], deep_at, deep_at]),
+        z_dim[1],
+        [r[3] for r in results],
+        [r[2] for r in results],
+        None,
+        None,
     )
     a = [keep_a, shifted(send_a, core_dims, 1)]
     dqs = [r[4] for r in results]
-    (send_b,) = weight_gradients(core, (1,), rows, dqs, text, dtext)
-    got_b = shifted(send_b, core_dims, 1)
-    (keep_b,) = weight_gradients(core, (0,), rows, dqs, text, dtext)
-    b = [keep_b, got_b]
+    send_b, keep_b = weight_gradients(
+        jnp.stack([core[0], at, other_at]), size, rows, dqs, text, dtext
+    )
+    b = [keep_b, shifted(send_b, core_dims, 1)]
     grad_text = dot_nt(dtext, projection_weight[:, width:]).astype(BF)
 
     heads = [r[0][:, :2] for r in results]
@@ -666,8 +705,8 @@
         axis=1,
     )
 
-    a = scatter_terms(a, deep)
-    b = scatter_terms(b, flat_first)
+    a = scatter_ready(a, deep)
+    b = scatter_ready(b, flat_first)
     b = scatter_terms(b, flat_second)
     a = scatter_terms(a, flat_first)
     b = scatter_terms(b, deep)
@@ -680,9 +719,6 @@
     b = gather_rows(b, flat_second)
     a = gather_rows(a, deep)
     other_a = shifted(a, core_dims, 1)
-    size = flat_first[0][1]
-    at = by_core(*flat_first)
-    other_at = by_core(flat_first[1], flat_first[0])
     pieces = [(core[0] * size + at, b)]
     pieces.append(((1 - core[0]) * size + other_at, shifted(b, core_dims, 1)))
     for k in range(1, size):
@@ -693,9 +729,9 @@
     grad_query = receive(requested, results[0][6], *returned)
     sum_qkv = None
     for place, piece in pieces:
-        sum_qkv = finish(place, piece, width, factor, sum_qkv)
-    sum_out = finish(core[0], a, width, factor, None)
-    sum_out = finish(1 - core[0], other_a, width, factor, sum_out)
+        sum_qkv = finish([place], [piece], width, factor, sum_qkv)
+    sum_out = finish([core[0]], [a], width, factor, None)
+    sum_out = finish([1 - core[0]], [other_a], width, factor, sum_out)
     return (
         logits,
         grad_text.reshape(captions, text_rows, width),

time: 276 us -> 253 us (0.917)
  waiting for transfers between devices: 67.5 us -> 49.9 us
  Pallas kernels: 99.5 us -> 86.7 us
  other arithmetic: 7.96 us -> 11.6 us
  local copies, waits for them, and re-layouts: 12.7 us -> 15.9 us
    ppermute x25, waiting for transfers between devices: 67.5 us -> 49.9 us  [shifted(): return lax.ppermute(x, 'dp', table)]
    pallas_call x3, Pallas kernels: 59.8 us -> 48.7 us  [pair_core(): pl.pallas_call(body, out_shape=out, in_specs=specs, out_specs=[vm] + [far...]
    slice x0 -> x4, local copies, waits for them, and re-layouts: none -> 3.79 us  [scatter_ready(): return [t[0] for t in split] + got]
    pallas_call x9 -> x8, Pallas kernels: 31.7 us -> 29.9 us  [the longest x2 16.8 us: weight_gradients(): pl.pallas_call(functools.partial(weight_kernel, size=size, groups=groups,...]
  transfers between devices with their start and end apart: 28 -> 28, of which waited for: 10 -> 10; matrix products, arithmetic and copies ran while one was open for 8% -> 12% of each run, Pallas kernels for 24% -> 21%
where the time goes in v1:
time: 253 us; the launch traced here: 251 us
  Pallas kernels  86.7 us (34%)
  waiting for transfers between devices  49.9 us (20%)
  starting transfers between devices  42.4 us (17%)
  blocking collectives  38.3 us (15%)
  local copies, waits for them, and re-layouts  15.9 us (6%)
  other arithmetic  11.6 us (5%)
  matrix products  5.4 us (2%)
    ppermute x25, waiting for transfers between devices, shifted(): return lax.ppermute(x, 'dp', table)  49.9 us
    pallas_call x3, Pallas kernels, pair_core(): pl.pallas_call(body, out_shape=out, in_specs=specs, out_specs=[vm] + [far...  48.7 us
    ppermute x25, starting transfers between devices, shifted(): return lax.ppermute(x, 'dp', table)  30.8 us
    all_to_all x1, blocking collectives, exchange(): moved = lax.all_to_all(split, 'dp', split_axis=0, concat_axis=0, tiled=True)  23.9 us
    pallas_call x2, Pallas kernels, weight_gradients(): pl.pallas_call(functools.partial(weight_kernel, size=size, groups=groups,...  16.8 us
    all_to_all x1, blocking collectives, step(): lax.all_to_all(wanted, 'dp', split_axis=0, concat_axis=0, tiled=True)  14.4 us
    pallas_call x6, Pallas kernels, finish(): pl.pallas_call(functools.partial(finish_kernel, count=n, factor=factor),...  13.1 us
    all_to_all x3, starting transfers between devices, exchange(): moved = lax.all_to_all(split, 'dp', split_axis=0, concat_axis=0, tiled=True)  11.6 us
  transfers between devices with their start and end apart: 28, of which 10 were waited for; matrix products, arithmetic and copies ran while one was open for 12% of the time, Pallas kernels for 21%

profile of v1, /device:TPU:0, one launch (start us, length us, event | category | flops | bytes accessed | tf_op | source)
XLA Modules:
  0.0 251.2 jit_solution(1741761209468027)
XLA Ops:
  2.0 2.0 route.1
  4.1 14.4 %all_to_all.31 = s32[32,1,2]{2,1,0:T(1,128)S(1)} all-to-all(s32[32,1,2]{2,1,0:T(1,128)} %bitcast.154), channel_id=1, replica_groups=mesh['dp'=32] {'dp'}, dimensions={0} | all-to-all | bytes 512 | tf_op jit(solution)/shard_map/all_to_all | solution.py:630
  19.3 2.5 give.1
  21.7 23.9 %all_to_all.32 = bf16[32,1,16,768]{3,2,1,0:T(8,128)(2,1)} all-to-all(bf16[32,1,16,768]{3,2,1,0:T(8,128)(2,1)} %bitcast.129), channel_id=1, replica_groups=mesh['dp'=32] {'dp'}, dimensions={0} | all-to-all | bytes 1572864 | tf_op jit(solution)/shard_map/all_to_all | solution.py:634
  45.6 3.7 %all-to-all-start.2 = ((bf16[32,1,16,768]{3,2,1,0:T(8,128)(2,1)}), bf16[32,1,16,768]{3,2,1,0:T(8,128)(2,1)}, u32[]{:S(2)}, u32[]{:S(2)}) async-start(bf16[32,1,16,768]{3,2,1,0:T(8,128)(2,1)} %bitcast.128), calls=%async_computation.2 | async-start | bytes 1572864 | tf_op jit(solution)/shard_map/all_to_all | solution.py:634
  50.6 2.7 %convolution_convert_fusion.refs_3_ = bf16[256,1536]{1,0:T(8,128)(2,1)} fusion(bf16[256,768]{1,0:T(8,128)(2,1)} %bitcast.136, bf16[768,2304]{1,0:T(8,128)(2,1)S(1)} %copy-done), kind=kOutput, calls=%fused_computation | convolution fusion | flops 604372992 | bytes 3538944 | tf_op jit(solution)/shard_map/dot_general | solution.py:20
  53.3 15.9 %pair_core.3 = (f32[16,128]{1,0:T(8,128)}, bf16[256,768]{1,0:T(8,128)(2,1)}, bf16[256,768]{1,0:T(8,128)(2,1)}, bf16[256,2304]{1,0:T(8,128)(2,1)}, f32[256,1536]{1,0:T(8,128)}, /*index=5*/f32[256,768]{1,0:T(8,128)}) custom-call(s32[16]{0:T(128)} %refs_0_.5, bf16[256,768]{1,0:T(8,128)(2,1)} %bitcast.110, bf16[768,2304]{1,0:T(8,128)(2,1)} %refs_2_.5, ...), custom_call_target="tpu_custom_call" | custom-call | tf_op jit(solution)/shard_map/pair_core/pallas_call | solution.py:275
  70.5 16.5 %pair_core.4 = (f32[16,128]{1,0:T(8,128)}, bf16[256,768]{1,0:T(8,128)(2,1)}, bf16[256,768]{1,0:T(8,128)(2,1)}, bf16[256,768]{1,0:T(8,128)(2,1)}, bf16[256,2304]{...) custom-call(s32[16]{0:T(128)} %refs_0_.5, bf16[512,768]{1,0:T(8,128)(2,1)} %bitcast.116, ...), custom_call_target="tpu_custom_call" | custom-call | tf_op jit(solution)/shard_map/pair_core/pallas_call | solution.py:275
  86.9 16.3 %pair_core.5 = (f32[16,128]{1,0:T(8,128)}, bf16[256,768]{1,0:T(8,128)(2,1)}, bf16[256,768]{1,0:T(8,128)(2,1)}, bf16[256,768]{1,0:T(8,128)(2,1)}, bf16[256,2304]{...) custom-call(s32[16]{0:T(128)} %refs_0_.5, bf16[512,768]{1,0:T(8,128)(2,1)} %bitcast.13.refs_1_, ...), custom_call_target="tpu_custom_call" | custom-call | tf_op jit(solution)/shard_map/pair_core/pallas_call | solution.py:275
  103.3 11.0 %weight_gradients.2 = (bf16[384,2304]{1,0:T(8,128)(2,1)}, bf16[384,2304]{1,0:T(8,128)(2,1)}) custom-call(s32[3]{0:T(128)} %pad_add_fusion.1.core, bf16[256,768]{1,0:T(8,128)(2,1)} %bitcast.111, bf16[256,768]{1,0:T(8,128)(2,1)} %get-tuple-element.48.refs_1_, bf16[256,768]{1,0:T(8,128)(2,1)} %get-tuple-element.49.refs_2_, ...), custom_call_target="tpu_custom_call" | custom-call | tf_op jit(solution)/shard_map/weight_gradients/pallas_call | solution.py:490
  115.2 5.8 %weight_gradients.3 = (bf16[384,768]{1,0:T(8,128)(2,1)}, bf16[384,768]{1,0:T(8,128)(2,1)}) custom-call(s32[3]{0:T(128)} %pad_add_fusion.2.core, bf16[256,768]{1,0:T(8,128)(2,1)} %get-tuple-element.55.refs_0_, bf16[256,768]{1,0:T(8,128)(2,1)} %get-tuple-element.56.refs_1_, bf16[256,768]{1,0:T(8,128)(2,1)} %get-tuple-element.57.refs_2_, ...), custom_call_target="tpu_custom_call" | custom-call | tf_op jit(solution)/shard_map/weight_gradients/pallas_call | solution.py:490
  126.6 2.4 collective-permute-start.16
  132.3 3.9 %all-to-all-start.3 = ((bf16[32,1,16,768]{3,2,1,0:T(8,128)(2,1)}), bf16[32,1,16,768]{3,2,1,0:T(8,128)(2,1)}, u32[]{:S(2)}, u32[]{:S(2)}) async-start(bf16[32,1,16,768]{3,2,1,0:T(8,128)(2,1)} %bitcast.127), calls=%async_computation.3 | async-start | bytes 1572864 | tf_op jit(solution)/shard_map/all_to_all | solution.py:634
  138.1 6.5 %collective-permute-done.15 = bf16[96,768]{1,0:T(8,128)(2,1)} collective-permute-done((bf16[96,768]{1,0:T(8,128)(2,1)}, bf16[96,768]{1,0:T(8,128)(2,1)}, u32[]{:S(2)}, u32[]{:S(2)}) %collective-permute-start.15) | collective-permute-done | bytes 147488 | tf_op jit(solution)/shard_map/ppermute | solution.py:567
  151.7 8.7 %collective-permute-done.2 = bf16[96,2304]{1,0:T(8,128)(2,1)S(1)} collective-permute-done((bf16[96,2304]{1,0:T(8,128)(2,1)S(1)}, bf16[96,2304]{1,0:T(8,128)(2,1)S(1)}, u32[]{:S(2)}, u32[]{:S(2)}) %collective-permute-start.2) | collective-permute-done | bytes 442400 | tf_op jit(solution)/shard_map/ppermute | solution.py:567
  161.5 3.4 %collective-permute-start.5 = (bf16[24,2304]{1,0:T(8,128)(2,1)S(1)}, bf16[24,2304]{1,0:T(8,128)(2,1)S(1)}, u32[]{:S(2)}, u32[]{:S(2)}) collective-permute-start(bf16[24,2304]{1,0:T(8,128)(2,1)S(1)} %get-tuple-element.66), channel_id=1, source_target_pairs={{0,24},{1,25},{2,26},{3,27},{4,28},{5,29},{6,30},{7,31},{8,0},{9,1... | collective-permute-start | bytes 331784 | tf_op jit(solution)/shard_map/ppermute | solution.py:567
  167.8 4.4 %collective-permute-done.4 = bf16[24,2304]{1,0:T(8,128)(2,1)S(1)} collective-permute-done((bf16[24,2304]{1,0:T(8,128)(2,1)S(1)}, bf16[24,2304]{1,0:T(8,128)(2,1)S(1)}, u32[]{:S(2)}, u32[]{:S(2)}) %collective-permute-start.4) | collective-permute-done | bytes 110624 | tf_op jit(solution)/shard_map/ppermute | solution.py:567
  174.0 3.4 %collective-permute-start.7 = (bf16[24,2304]{1,0:T(8,128)(2,1)S(1)}, bf16[24,2304]{1,0:T(8,128)(2,1)S(1)}, u32[]{:S(2)}, u32[]{:S(2)}) collective-permute-start(bf16[24,2304]{1,0:T(8,128)(2,1)S(1)} %get-tuple-element.64), channel_id=1, source_target_pairs={{0,16},{1,17},{2,18},{3,19},{4,20},{5,21},{6,22},{7,23},{8,24},{9,... | collective-permute-start | bytes 331784 | tf_op jit(solution)/shard_map/ppermute | solution.py:567
  179.1 3.2 %collective-permute-done.7 = bf16[24,2304]{1,0:T(8,128)(2,1)S(1)} collective-permute-done((bf16[24,2304]{1,0:T(8,128)(2,1)S(1)}, bf16[24,2304]{1,0:T(8,128)(2,1)S(1)}, u32[]{:S(2)}, u32[]{:S(2)}) %collective-permute-start.7) | collective-permute-done | bytes 110624 | tf_op jit(solution)/shard_map/ppermute | solution.py:567
  185.8 2.9 %collective-permute-done.20 = bf16[48,768]{1,0:T(8,128)(2,1)S(1)} collective-permute-done((bf16[48,768]{1,0:T(8,128)(2,1)S(1)}, bf16[48,768]{1,0:T(8,128)(2,1)S(1)}, u32[]{:S(2)}, u32[]{:S(2)}) %collective-permute-start.20) | collective-permute-done | bytes 73760 | tf_op jit(solution)/shard_map/ppermute | solution.py:567
  188.7 3.0 %collective-permute-done.9 = bf16[96,2304]{1,0:T(8,128)(2,1)S(1)} collective-permute-done((bf16[96,2304]{1,0:T(8,128)(2,1)S(1)}, bf16[96,2304]{1,0:T(8,128)(2,1)S(1)}, u32[]{:S(2)}, u32[]{:S(2)}) %collective-permute-start.9) | collective-permute-done | bytes 442400 | tf_op jit(solution)/shard_map/ppermute | solution.py:567
  195.7 4.0 %all-to-all-start.4 = ((bf16[32,1,16,768]{3,2,1,0:T(8,128)(2,1)}), bf16[32,1,16,768]{3,2,1,0:T(8,128)(2,1)}, u32[]{:S(2)}, u32[]{:S(2)}) async-start(bf16[32,1,16,768]{3,2,1,0:T(8,128)(2,1)} %bitcast.126), calls=%async_computation.4 | async-start | bytes 1572864 | tf_op jit(solution)/shard_map/all_to_all | solution.py:634
  200.9 2.6 %collective-permute-start.22 = (bf16[96,768]{1,0:T(8,128)(2,1)}, bf16[96,768]{1,0:T(8,128)(2,1)S(1)}, u32[]{:S(2)}, u32[]{:S(2)}) collective-permute-start(bf16[96,768]{1,0:T(8,128)(2,1)} %pad_maximum_fusion.1), channel_id=1, source_target_pairs={{0,16},{1,17},{2,18},{3,19},{4,20},{5,21},{6,22},{7,23},{8,24},{9,... | collective-permute-start | bytes 442376 | tf_op jit(solution)/shard_map/ppermute | solution.py:567
  209.0 18.1 %collective-permute-done.22 = bf16[96,768]{1,0:T(8,128)(2,1)S(1)} collective-permute-done((bf16[96,768]{1,0:T(8,128)(2,1)}, bf16[96,768]{1,0:T(8,128)(2,1)S(1)}, u32[]{:S(2)}, u32[]{:S(2)}) %collective-permute-start.22) | collective-permute-done | bytes 147488 | tf_op jit(solution)/shard_map/ppermute | solution.py:567
  231.8 2.7 %fusion.3 = bf16[256,768]{1,0:T(8,128)(2,1)} fusion(bf16[256,1536]{1,0:T(8,128)(2,1)} %get-tuple-element.44.refs_7_, bf16[768,2304]{1,0:T(8,128)(2,1)S(1)} %copy-done.1), kind=kOutput, calls=%fused_computation.5 | convolution fusion | flops 604176384 | bytes 3538944 | tf_op jit(solution)/shard_map/dot_general | solution.py:16
  234.5 2.0 finish.10.refs_1_
  236.5 3.5 %receive.1 = bf16[256,768]{1,0:T(8,128)(2,1)} custom-call(s32[32,2]{1,0:T(8,128)} %copy.33.wanted, f32[256,768]{1,0:T(8,128)} %get-tuple-element.45.own, bf16[512,768]{1,0:T(8,128)(2,1)} %bitcast.20.first, bf16[512,768]{1,0:T(8,128)(2,1)} %bitcast.23.second), custom_call_target="tpu_custom_call" | custom-call | tf_op jit(solution)/shard_map/receive/pallas_call | solution.py:341
  240.1 2.0 finish.11
  242.1 2.3 finish.6.refs_1_
  244.3 2.3 finish.7.refs_1_
  246.6 2.3 finish.8.refs_1_
  248.9 2.3 finish.9
  (116 shorter events, 49.6 us)
Async XLA Ops:
  19.3 30.1 %copy-start.8 = (f32[768]{0:T(1024)S(1)}, f32[768]{0:T(1024)}, u32[]{:S(2)}) copy-start(f32[768]{0:T(1024)} %param.18) | copy-start | bytes 9220
  19.3 30.7 %copy-start.9 = (f32[768]{0:T(1024)S(1)}, f32[768]{0:T(1024)}, u32[]{:S(2)}) copy-start(f32[768]{0:T(1024)} %param.19) | copy-start | bytes 9220
  19.3 31.3 %copy-start = (bf16[768,2304]{1,0:T(8,128)(2,1)S(1)}, bf16[768,2304]{1,0:T(8,128)(2,1)}, u32[]{:S(2)}) copy-start(bf16[768,2304]{1,0:T(8,128)(2,1)} %refs_2_.5) | copy-start | bytes 10616836
  45.6 41.3 %all-to-all-start.2 = ((bf16[32,1,16,768]{3,2,1,0:T(8,128)(2,1)}), bf16[32,1,16,768]{3,2,1,0:T(8,128)(2,1)}, u32[]{:S(2)}, u32[]{:S(2)}) async-start(bf16[32,1,16,768]{3,2,1,0:T(8,128)(2,1)} %bitcast.128), calls=%async_computation.2 | async-start | bytes 1572864 | tf_op jit(solution)/shard_map/all_to_all | solution.py:634
  114.2 7.1 %collective-permute-start = (bf16[384,2304]{1,0:T(8,128)(2,1)}, bf16[384,2304]{1,0:T(8,128)(2,1)S(1)}, u32[]{:S(2)}, u32[]{:S(2)}) collective-permute-start(bf16[384,2304]{1,0:T(8,128)(2,1)} %get-tuple-element.54), channel_id=1, source_target_pairs={{0,1},{1,0},{2,3},{3,2},{4,5},{5,4},{6,7},{7,6},{8,9},{9,8},{10,11... | collective-permute-start | bytes 5308424 | tf_op jit(solution)/shard_map/ppermute | solution.py:567
  121.0 3.1 %collective-permute-start.13 = (bf16[384,768]{1,0:T(8,128)(2,1)}, bf16[384,768]{1,0:T(8,128)(2,1)S(1)}, u32[]{:S(2)}, u32[]{:S(2)}) collective-permute-start(bf16[384,768]{1,0:T(8,128)(2,1)} %get-tuple-element.62), channel_id=1, source_target_pairs={{0,1},{1,0},{2,3},{3,2},{4,5},{5,4},{6,7},{7,6},{8,9},{9,8},{10,11... | collective-permute-start | bytes 1769480 | tf_op jit(solution)/shard_map/ppermute | solution.py:567
  122.4 27.9 %collective-permute-start.1 = (bf16[192,2304]{1,0:T(8,128)(2,1)}, bf16[192,2304]{1,0:T(8,128)(2,1)S(1)}, u32[]{:S(2)}, u32[]{:S(2)}) collective-permute-start(bf16[192,2304]{1,0:T(8,128)(2,1)} %add_convert_fusion), channel_id=1, source_target_pairs={{0,2},{1,5},{2,0},{3,7},{4,6},{5,1},{6,4},{7,3},{8,10},{9,13},{10,... | collective-permute-start | bytes 2654216 | tf_op jit(solution)/shard_map/ppermute | solution.py:567
  125.1 12.9 %collective-permute-start.14 = (bf16[96,768]{1,0:T(8,128)(2,1)}, bf16[96,768]{1,0:T(8,128)(2,1)}, u32[]{:S(2)}, u32[]{:S(2)}) collective-permute-start(bf16[96,768]{1,0:T(8,128)(2,1)} %get-tuple-element.68), channel_id=1, source_target_pairs={{0,8},{1,9},{2,10},{3,11},{4,12},{5,13},{6,14},{7,15},{8,16},{9,17... | collective-permute-start | bytes 442376 | tf_op jit(solution)/shard_map/ppermute | solution.py:567
  126.6 11.5 %collective-permute-start.16 = (bf16[96,768]{1,0:T(8,128)(2,1)}, bf16[96,768]{1,0:T(8,128)(2,1)}, u32[]{:S(2)}, u32[]{:S(2)}) collective-permute-start(bf16[96,768]{1,0:T(8,128)(2,1)} %get-tuple-element.69), channel_id=1, source_target_pairs={{0,24},{1,25},{2,26},{3,27},{4,28},{5,29},{6,30},{7,31},{8,0},{9,1... | collective-permute-start | bytes 442376 | tf_op jit(solution)/shard_map/ppermute | solution.py:567
  128.9 15.6 %collective-permute-start.15 = (bf16[96,768]{1,0:T(8,128)(2,1)}, bf16[96,768]{1,0:T(8,128)(2,1)}, u32[]{:S(2)}, u32[]{:S(2)}) collective-permute-start(bf16[96,768]{1,0:T(8,128)(2,1)} %get-tuple-element.70), channel_id=1, source_target_pairs={{0,16},{1,17},{2,18},{3,19},{4,20},{5,21},{6,22},{7,23},{8,24},{9,... | collective-permute-start | bytes 442376 | tf_op jit(solution)/shard_map/ppermute | solution.py:567
  132.3 63.4 %all-to-all-start.3 = ((bf16[32,1,16,768]{3,2,1,0:T(8,128)(2,1)}), bf16[32,1,16,768]{3,2,1,0:T(8,128)(2,1)}, u32[]{:S(2)}, u32[]{:S(2)}) async-start(bf16[32,1,16,768]{3,2,1,0:T(8,128)(2,1)} %bitcast.127), calls=%async_computation.3 | async-start | bytes 1572864 | tf_op jit(solution)/shard_map/all_to_all | solution.py:634
  145.6 19.8 %collective-permute-start.17 = (bf16[48,768]{1,0:T(8,128)(2,1)S(1)}, bf16[48,768]{1,0:T(8,128)(2,1)S(1)}, u32[]{:S(2)}, u32[]{:S(2)}) collective-permute-start(bf16[48,768]{1,0:T(8,128)(2,1)S(1)} %fusion.13), channel_id=1, source_target_pairs={{0,2},{1,5},{2,0},{3,7},{4,6},{5,1},{6,4},{7,3},{8,10},{9,13},{10,... | collective-permute-start | bytes 221192 | tf_op jit(solution)/shard_map/ppermute | solution.py:567
  150.5 9.9 %collective-permute-start.2 = (bf16[96,2304]{1,0:T(8,128)(2,1)S(1)}, bf16[96,2304]{1,0:T(8,128)(2,1)S(1)}, u32[]{:S(2)}, u32[]{:S(2)}) collective-permute-start(bf16[96,2304]{1,0:T(8,128)(2,1)S(1)} %fusion.6), channel_id=1, source_target_pairs={{0,4},{1,3},{2,6},{3,1},{4,0},{5,7},{6,2},{7,5},{8,12},{9,11},{10,... | collective-permute-start | bytes 1327112 | tf_op jit(solution)/shard_map/ppermute | solution.py:567
  160.6 7.2 %collective-permute-start.3 = (bf16[24,2304]{1,0:T(8,128)(2,1)S(1)}, bf16[24,2304]{1,0:T(8,128)(2,1)S(1)}, u32[]{:S(2)}, u32[]{:S(2)}) collective-permute-start(bf16[24,2304]{1,0:T(8,128)(2,1)S(1)} %get-tuple-element.65), channel_id=1, source_target_pairs={{0,8},{1,9},{2,10},{3,11},{4,12},{5,13},{6,14},{7,15},{8,16},{9,17... | collective-permute-start | bytes 331784 | tf_op jit(solution)/shard_map/ppermute | solution.py:567
  161.5 6.3 %collective-permute-start.5 = (bf16[24,2304]{1,0:T(8,128)(2,1)S(1)}, bf16[24,2304]{1,0:T(8,128)(2,1)S(1)}, u32[]{:S(2)}, u32[]{:S(2)}) collective-permute-start(bf16[24,2304]{1,0:T(8,128)(2,1)S(1)} %get-tuple-element.66), channel_id=1, source_target_pairs={{0,24},{1,25},{2,26},{3,27},{4,28},{5,29},{6,30},{7,31},{8,0},{9,1... | collective-permute-start | bytes 331784 | tf_op jit(solution)/shard_map/ppermute | solution.py:567
  164.9 7.3 %collective-permute-start.4 = (bf16[24,2304]{1,0:T(8,128)(2,1)S(1)}, bf16[24,2304]{1,0:T(8,128)(2,1)S(1)}, u32[]{:S(2)}, u32[]{:S(2)}) collective-permute-start(bf16[24,2304]{1,0:T(8,128)(2,1)S(1)} %get-tuple-element.67), channel_id=1, source_target_pairs={{0,16},{1,17},{2,18},{3,19},{4,20},{5,21},{6,22},{7,23},{8,24},{9,... | collective-permute-start | bytes 331784 | tf_op jit(solution)/shard_map/ppermute | solution.py:567
  165.5 7.0 %collective-permute-start.18 = (bf16[24,768]{1,0:T(8,128)(2,1)S(1)}, bf16[24,768]{1,0:T(8,128)(2,1)S(1)}, u32[]{:S(2)}, u32[]{:S(2)}) collective-permute-start(bf16[24,768]{1,0:T(8,128)(2,1)S(1)} %fusion.15), channel_id=1, source_target_pairs={{0,4},{1,3},{2,6},{3,1},{4,0},{5,7},{6,2},{7,5},{8,12},{9,11},{10,... | collective-permute-start | bytes 110600 | tf_op jit(solution)/shard_map/ppermute | solution.py:567
  172.4 6.7 %collective-permute-start.6 = (bf16[24,2304]{1,0:T(8,128)(2,1)S(1)}, bf16[24,2304]{1,0:T(8,128)(2,1)S(1)}, u32[]{:S(2)}, u32[]{:S(2)}) collective-permute-start(bf16[24,2304]{1,0:T(8,128)(2,1)S(1)} %get-tuple-element.64), channel_id=1, source_target_pairs={{0,8},{1,9},{2,10},{3,11},{4,12},{5,13},{6,14},{7,15},{8,16},{9,17... | collective-permute-start | bytes 331784 | tf_op jit(solution)/shard_map/ppermute | solution.py:567
  172.5 11.7 %collective-permute-start.19 = (bf16[24,768]{1,0:T(8,128)(2,1)S(1)}, bf16[24,768]{1,0:T(8,128)(2,1)S(1)}, u32[]{:S(2)}, u32[]{:S(2)}) collective-permute-start(bf16[24,768]{1,0:T(8,128)(2,1)S(1)} %fusion.14), channel_id=1, source_target_pairs={{0,4},{1,3},{2,6},{3,1},{4,0},{5,7},{6,2},{7,5},{8,12},{9,11},{10,... | collective-permute-start | bytes 110600 | tf_op jit(solution)/shard_map/ppermute | solution.py:567
  174.0 8.4 %collective-permute-start.7 = (bf16[24,2304]{1,0:T(8,128)(2,1)S(1)}, bf16[24,2304]{1,0:T(8,128)(2,1)S(1)}, u32[]{:S(2)}, u32[]{:S(2)}) collective-permute-start(bf16[24,2304]{1,0:T(8,128)(2,1)S(1)} %get-tuple-element.64), channel_id=1, source_target_pairs={{0,16},{1,17},{2,18},{3,19},{4,20},{5,21},{6,22},{7,23},{8,24},{9,... | collective-permute-start | bytes 331784 | tf_op jit(solution)/shard_map/ppermute | solution.py:567
  177.4 5.6 %collective-permute-start.8 = (bf16[24,2304]{1,0:T(8,128)(2,1)S(1)}, bf16[24,2304]{1,0:T(8,128)(2,1)S(1)}, u32[]{:S(2)}, u32[]{:S(2)}) collective-permute-start(bf16[24,2304]{1,0:T(8,128)(2,1)S(1)} %get-tuple-element.64), channel_id=1, source_target_pairs={{0,24},{1,25},{2,26},{3,27},{4,28},{5,29},{6,30},{7,31},{8,0},{9,1... | collective-permute-start | bytes 331784 | tf_op jit(solution)/shard_map/ppermute | solution.py:567
  183.0 8.7 %collective-permute-start.9 = (bf16[96,2304]{1,0:T(8,128)(2,1)S(1)}, bf16[96,2304]{1,0:T(8,128)(2,1)S(1)}, u32[]{:S(2)}, u32[]{:S(2)}) collective-permute-start(bf16[96,2304]{1,0:T(8,128)(2,1)S(1)} %bitcast.123), channel_id=1, source_target_pairs={{0,4},{1,3},{2,6},{3,1},{4,0},{5,7},{6,2},{7,5},{8,12},{9,11},{10,... | collective-permute-start | bytes 1327112 | tf_op jit(solution)/shard_map/ppermute | solution.py:567
  184.3 4.4 %collective-permute-start.20 = (bf16[48,768]{1,0:T(8,128)(2,1)S(1)}, bf16[48,768]{1,0:T(8,128)(2,1)S(1)}, u32[]{:S(2)}, u32[]{:S(2)}) collective-permute-start(bf16[48,768]{1,0:T(8,128)(2,1)S(1)} %pad_maximum_fusion.2), channel_id=1, source_target_pairs={{0,2},{1,5},{2,0},{3,7},{4,6},{5,1},{6,4},{7,3},{8,10},{9,13},{10,... | collective-permute-start | bytes 221192 | tf_op jit(solution)/shard_map/ppermute | solution.py:567
  192.8 35.0 %collective-permute-start.10 = (bf16[192,2304]{1,0:T(8,128)(2,1)}, bf16[192,2304]{1,0:T(8,128)(2,1)}, u32[]{:S(2)}, u32[]{:S(2)}) collective-permute-start(bf16[192,2304]{1,0:T(8,128)(2,1)} %pad_maximum_fusion.refs_0_), channel_id=1, source_target_pairs={{0,2},{1,5},{2,0},{3,7},{4,6},{5,1},{6,4},{7,3},{8,10},{9,13},{10,... | collective-permute-start | bytes 2654216 | tf_op jit(solution)/shard_map/ppermute | solution.py:567
  193.1 38.7 %copy-start.1 = (bf16[768,2304]{1,0:T(8,128)(2,1)S(1)}, bf16[768,2304]{1,0:T(8,128)(2,1)}, u32[]{:S(2)}) copy-start(bf16[768,2304]{1,0:T(8,128)(2,1)} %refs_2_.5) | copy-start | bytes 10616836
  193.8 13.6 %collective-permute-start.21 = (bf16[96,768]{1,0:T(8,128)(2,1)}, bf16[96,768]{1,0:T(8,128)(2,1)}, u32[]{:S(2)}, u32[]{:S(2)}) collective-permute-start(bf16[96,768]{1,0:T(8,128)(2,1)} %pad_maximum_fusion.1), channel_id=1, source_target_pairs={{0,8},{1,9},{2,10},{3,11},{4,12},{5,13},{6,14},{7,15},{8,16},{9,17... | collective-permute-start | bytes 442376 | tf_op jit(solution)/shard_map/ppermute | solution.py:567
  195.7 40.8 %all-to-all-start.4 = ((bf16[32,1,16,768]{3,2,1,0:T(8,128)(2,1)}), bf16[32,1,16,768]{3,2,1,0:T(8,128)(2,1)}, u32[]{:S(2)}, u32[]{:S(2)}) async-start(bf16[32,1,16,768]{3,2,1,0:T(8,128)(2,1)} %bitcast.126), calls=%async_computation.4 | async-start | bytes 1572864 | tf_op jit(solution)/shard_map/all_to_all | solution.py:634
  200.9 26.2 %collective-permute-start.22 = (bf16[96,768]{1,0:T(8,128)(2,1)}, bf16[96,768]{1,0:T(8,128)(2,1)S(1)}, u32[]{:S(2)}, u32[]{:S(2)}) collective-permute-start(bf16[96,768]{1,0:T(8,128)(2,1)} %pad_maximum_fusion.1), channel_id=1, source_target_pairs={{0,16},{1,17},{2,18},{3,19},{4,20},{5,21},{6,22},{7,23},{8,24},{9,... | collective-permute-start | bytes 442376 | tf_op jit(solution)/shard_map/ppermute | solution.py:567
  203.5 24.8 %collective-permute-start.23 = (bf16[96,768]{1,0:T(8,128)(2,1)}, bf16[96,768]{1,0:T(8,128)(2,1)S(1)}, u32[]{:S(2)}, u32[]{:S(2)}) collective-permute-start(bf16[96,768]{1,0:T(8,128)(2,1)} %pad_maximum_fusion.1), channel_id=1, source_target_pairs={{0,24},{1,25},{2,26},{3,27},{4,28},{5,29},{6,30},{7,31},{8,0},{9,1... | collective-permute-start | bytes 442376 | tf_op jit(solution)/shard_map/ppermute | solution.py:567
  227.8 16.5 %collective-permute-start.12 = (bf16[192,2304]{1,0:T(8,128)(2,1)}, bf16[192,2304]{1,0:T(8,128)(2,1)}, u32[]{:S(2)}, u32[]{:S(2)}) collective-permute-start(bf16[192,2304]{1,0:T(8,128)(2,1)} %pad_maximum_fusion.refs_0_), channel_id=1, source_target_pairs={{0,1},{1,0},{2,3},{3,2},{4,5},{5,4},{6,7},{7,6},{8,9},{9,8},{10,11... | collective-permute-start | bytes 2654216 | tf_op jit(solution)/shard_map/ppermute | solution.py:567
  227.8 21.1 %collective-permute-start.11 = (bf16[192,2304]{1,0:T(8,128)(2,1)}, bf16[192,2304]{1,0:T(8,128)(2,1)}, u32[]{:S(2)}, u32[]{:S(2)}) collective-permute-start(bf16[192,2304]{1,0:T(8,128)(2,1)} %collective-permute-done.10.refs_0_), channel_id=1, source_target_pairs={{0,1},{1,0},{2,3},{3,2},{4,5},{5,4},{6,7},{7,6},{8,9},{9,8},{10,11... | collective-permute-start | bytes 2654216 | tf_op jit(solution)/shard_map/ppermute | solution.py:567
  229.0 11.0 %collective-permute-start.24 = (bf16[384,768]{1,0:T(8,128)(2,1)}, bf16[384,768]{1,0:T(8,128)(2,1)}, u32[]{:S(2)}, u32[]{:S(2)}) collective-permute-start(bf16[384,768]{1,0:T(8,128)(2,1)} %bitcast.69.refs_0_), channel_id=1, source_target_pairs={{0,1},{1,0},{2,3},{3,2},{4,5},{5,4},{6,7},{7,6},{8,9},{9,8},{10,11... | collective-permute-start | bytes 1769480 | tf_op jit(solution)/shard_map/ppermute | solution.py:567
  (9 other events, 81.2 us)

commit v2 on v1

--- a/solution.py
+++ b/solution.py
@@ -728,10 +728,15 @@
         pieces.append(((1 - core[0]) * size + (other_at - k) % size, got))
     grad_query = receive(requested, results[0][6], *returned)
     sum_qkv = None
-    for place, piece in pieces:
-        sum_qkv = finish([place], [piece], width, factor, sum_qkv)
+    for i, (place, piece) in enumerate(pieces):
+        if i == 0:
+            sum_qkv = finish([place], [piece], width, factor, None)
+        else:
+            scaled = piece.astype(F32) * factor
+            sum_qkv = lax.dynamic_update_slice(sum_qkv, scaled, (place * piece.shape[0], 0))
     sum_out = finish([core[0]], [a], width, factor, None)
-    sum_out = finish([1 - core[0]], [other_a], width, factor, sum_out)
+    scaled = other_a.astype(F32) * factor
+    sum_out = lax.dynamic_update_slice(sum_out, scaled, ((1 - core[0]) * a.shape[0], 0))
     return (
         logits,
         grad_text.reshape(captions, text_rows, width),

time: 253 us -> 261 us (1.032)
  other arithmetic: 11.6 us -> 21.9 us
  Pallas kernels: 86.7 us -> 78.6 us
  waiting for transfers between devices: 49.9 us -> 54.4 us
  starting transfers between devices: 42.4 us -> 46.1 us
    all_to_all x3, waiting for transfers between devices: 0.01 us -> 8.89 us  [exchange(): moved = lax.all_to_all(split, 'dp', split_axis=0, concat_axis=0, tiled=True)]
    pallas_call x6 -> x2, Pallas kernels: 13.1 us -> 4.8 us  [finish(): pl.pallas_call(functools.partial(finish_kernel, count=n, factor=factor),...]
    dynamic_update_slice x0 -> x4, other arithmetic: none -> 7.46 us  [the longest x3 6.31 us: step(): lax.dynamic_update_slice(sum_qkv, scaled, (place * piece.shape[0], 0))]
    ppermute x25, waiting for transfers between devices: 49.9 us -> 45.5 us  [shifted(): return lax.ppermute(x, 'dp', table)]
    all_to_all x3, starting transfers between devices: 11.6 us -> 14.2 us  [exchange(): moved = lax.all_to_all(split, 'dp', split_axis=0, concat_axis=0, tiled=True)]
  transfers between devices with their start and end apart: 28 -> 28, of which waited for: 10 -> 10; matrix products, arithmetic and copies ran while one was open for 12% -> 14% of each run, Pallas kernels for 21% -> 20%
where the time goes in v2:
time: 261 us; the launch traced here: 259 us
  Pallas kernels  78.6 us (30%)
  waiting for transfers between devices  54.4 us (21%)
  starting transfers between devices  46.1 us (18%)
  blocking collectives  38.3 us (15%)
  other arithmetic  21.9 us (8%)
  local copies, waits for them, and re-layouts  13.5 us (5%)
  matrix products  5.38 us (2%)
    pallas_call x3, Pallas kernels, pair_core(): pl.pallas_call(body, out_shape=out, in_specs=specs, out_specs=[vm] + [far...  48.7 us
    ppermute x25, waiting for transfers between devices, shifted(): return lax.ppermute(x, 'dp', table)  45.5 us
    ppermute x25, starting transfers between devices, shifted(): return lax.ppermute(x, 'dp', table)  31.9 us
    all_to_all x1, blocking collectives, exchange(): moved = lax.all_to_all(split, 'dp', split_axis=0, concat_axis=0, tiled=True)  23.9 us
    pallas_call x2, Pallas kernels, weight_gradients(): pl.pallas_call(functools.partial(weight_kernel, size=size, groups=groups,...  17 us
    all_to_all x1, blocking collectives, step(): lax.all_to_all(wanted, 'dp', split_axis=0, concat_axis=0, tiled=True)  14.4 us
    all_to_all x3, starting transfers between devices, exchange(): moved = lax.all_to_all(split, 'dp', split_axis=0, concat_axis=0, tiled=True)  14.2 us
    all_to_all x3, waiting for transfers between devices, exchange(): moved = lax.all_to_all(split, 'dp', split_axis=0, concat_axis=0, tiled=True)  8.89 us
  transfers between devices with their start and end apart: 28, of which 10 were waited for; matrix products, arithmetic and copies ran while one was open for 14% of the time, Pallas kernels for 20%

profile of v2, /device:TPU:0, one launch (start us, length us, event | category | flops | bytes accessed | tf_op | source)
XLA Modules:
  0.0 259.2 jit_solution(2633524533772349257)
XLA Ops:
  4.1 14.4 %all_to_all.31 = s32[32,1,2]{2,1,0:T(1,128)S(1)} all-to-all(s32[32,1,2]{2,1,0:T(1,128)} %bitcast.153), channel_id=1, replica_groups=mesh['dp'=32] {'dp'}, dimensions={0} | all-to-all | bytes 512 | tf_op jit(solution)/shard_map/all_to_all | solution.py:630
  19.3 2.4 give.1
  21.7 23.9 %all_to_all.32 = bf16[32,1,16,768]{3,2,1,0:T(8,128)(2,1)} all-to-all(bf16[32,1,16,768]{3,2,1,0:T(8,128)(2,1)} %bitcast.122), channel_id=1, replica_groups=mesh['dp'=32] {'dp'}, dimensions={0} | all-to-all | bytes 1572864 | tf_op jit(solution)/shard_map/all_to_all | solution.py:634
  45.6 3.7 %all-to-all-start.2 = ((bf16[32,1,16,768]{3,2,1,0:T(8,128)(2,1)}), bf16[32,1,16,768]{3,2,1,0:T(8,128)(2,1)}, u32[]{:S(2)}, u32[]{:S(2)}) async-start(bf16[32,1,16,768]{3,2,1,0:T(8,128)(2,1)} %bitcast.121), calls=%async_computation.2 | async-start | bytes 1572864 | tf_op jit(solution)/shard_map/all_to_all | solution.py:634
  50.6 2.7 %convolution_convert_fusion.refs_3_ = bf16[256,1536]{1,0:T(8,128)(2,1)} fusion(bf16[256,768]{1,0:T(8,128)(2,1)} %bitcast.129, bf16[768,2304]{1,0:T(8,128)(2,1)S(1)} %copy-done), kind=kOutput, calls=%fused_computation | convolution fusion | flops 604372992 | bytes 3538944 | tf_op jit(solution)/shard_map/dot_general | solution.py:20
  53.3 15.9 %pair_core.3 = (f32[16,128]{1,0:T(8,128)}, bf16[256,768]{1,0:T(8,128)(2,1)}, bf16[256,768]{1,0:T(8,128)(2,1)}, bf16[256,2304]{1,0:T(8,128)(2,1)}, f32[256,1536]{1,0:T(8,128)}, /*index=5*/f32[256,768]{1,0:T(8,128)}) custom-call(s32[16]{0:T(128)} %refs_0_.5, bf16[256,768]{1,0:T(8,128)(2,1)} %bitcast.106, bf16[768,2304]{1,0:T(8,128)(2,1)} %refs_2_.5, ...), custom_call_target="tpu_custom_call" | custom-call | tf_op jit(solution)/shard_map/pair_core/pallas_call | solution.py:275
  70.4 16.5 %pair_core.4 = (f32[16,128]{1,0:T(8,128)}, bf16[256,768]{1,0:T(8,128)(2,1)}, bf16[256,768]{1,0:T(8,128)(2,1)}, bf16[256,768]{1,0:T(8,128)(2,1)}, bf16[256,2304]{...) custom-call(s32[16]{0:T(128)} %refs_0_.5, bf16[512,768]{1,0:T(8,128)(2,1)} %bitcast.112, ...), custom_call_target="tpu_custom_call" | custom-call | tf_op jit(solution)/shard_map/pair_core/pallas_call | solution.py:275
  86.9 16.3 %pair_core.5 = (f32[16,128]{1,0:T(8,128)}, bf16[256,768]{1,0:T(8,128)(2,1)}, bf16[256,768]{1,0:T(8,128)(2,1)}, bf16[256,768]{1,0:T(8,128)(2,1)}, bf16[256,2304]{...) custom-call(s32[16]{0:T(128)} %refs_0_.5, bf16[512,768]{1,0:T(8,128)(2,1)} %bitcast.13.refs_1_, ...), custom_call_target="tpu_custom_call" | custom-call | tf_op jit(solution)/shard_map/pair_core/pallas_call | solution.py:275
  103.2 5.9 %weight_gradients.3 = (bf16[384,768]{1,0:T(8,128)(2,1)}, bf16[384,768]{1,0:T(8,128)(2,1)}) custom-call(s32[3]{0:T(128)} %pad_add_fusion.2.core, bf16[256,768]{1,0:T(8,128)(2,1)} %get-tuple-element.55.refs_0_, bf16[256,768]{1,0:T(8,128)(2,1)} %get-tuple-element.56.refs_1_, bf16[256,768]{1,0:T(8,128)(2,1)} %get-tuple-element.57.refs_2_, ...), custom_call_target="tpu_custom_call" | custom-call | tf_op jit(solution)/shard_map/weight_gradients/pallas_call | solution.py:490
  109.9 11.1 %weight_gradients.2 = (bf16[384,2304]{1,0:T(8,128)(2,1)}, bf16[384,2304]{1,0:T(8,128)(2,1)}) custom-call(s32[3]{0:T(128)} %pad_add_fusion.1.core, bf16[256,768]{1,0:T(8,128)(2,1)} %bitcast.107, bf16[256,768]{1,0:T(8,128)(2,1)} %get-tuple-element.48.refs_1_, bf16[256,768]{1,0:T(8,128)(2,1)} %get-tuple-element.49.refs_2_, ...), custom_call_target="tpu_custom_call" | custom-call | tf_op jit(solution)/shard_map/weight_gradients/pallas_call | solution.py:490
  122.2 3.6 %collective-permute-start.16 = (bf16[96,768]{1,0:T(8,128)(2,1)}, bf16[96,768]{1,0:T(8,128)(2,1)S(1)}, u32[]{:S(2)}, u32[]{:S(2)}) collective-permute-start(bf16[96,768]{1,0:T(8,128)(2,1)} %get-tuple-element.69), channel_id=1, source_target_pairs={{0,24},{1,25},{2,26},{3,27},{4,28},{5,29},{6,30},{7,31},{8,0},{9,1... | collective-permute-start | bytes 442376 | tf_op jit(solution)/shard_map/ppermute | solution.py:567
  126.9 3.5 %collective-permute-done.16 = bf16[96,768]{1,0:T(8,128)(2,1)S(1)} collective-permute-done((bf16[96,768]{1,0:T(8,128)(2,1)}, bf16[96,768]{1,0:T(8,128)(2,1)S(1)}, u32[]{:S(2)}, u32[]{:S(2)}) %collective-permute-start.16) | collective-permute-done | bytes 147488 | tf_op jit(solution)/shard_map/ppermute | solution.py:567
  130.4 8.5 %collective-permute-done.15 = bf16[96,768]{1,0:T(8,128)(2,1)S(1)} collective-permute-done((bf16[96,768]{1,0:T(8,128)(2,1)}, bf16[96,768]{1,0:T(8,128)(2,1)S(1)}, u32[]{:S(2)}, u32[]{:S(2)}) %collective-permute-start.15) | collective-permute-done | bytes 147488 | tf_op jit(solution)/shard_map/ppermute | solution.py:567
  140.5 2.9 %collective-permute-done.17 = bf16[48,768]{1,0:T(8,128)(2,1)S(1)} collective-permute-done((bf16[48,768]{1,0:T(8,128)(2,1)S(1)}, bf16[48,768]{1,0:T(8,128)(2,1)S(1)}, u32[]{:S(2)}, u32[]{:S(2)}) %collective-permute-start.17) | collective-permute-done | bytes 73760 | tf_op jit(solution)/shard_map/ppermute | solution.py:567
  145.0 2.5 collective-permute-done.18
  149.0 2.3 add_convert_fusion
  156.4 4.0 %all-to-all-start.3 = ((bf16[32,1,16,768]{3,2,1,0:T(8,128)(2,1)}), bf16[32,1,16,768]{3,2,1,0:T(8,128)(2,1)S(1)}, u32[]{:S(2)}, u32[]{:S(2)}) async-start(bf16[32,1,16,768]{3,2,1,0:T(8,128)(2,1)} %bitcast.120), calls=%async_computation.3 | async-start | bytes 1572864 | tf_op jit(solution)/shard_map/all_to_all | solution.py:634
  160.4 9.7 %collective-permute-done.20 = bf16[48,768]{1,0:T(8,128)(2,1)} collective-permute-done((bf16[48,768]{1,0:T(8,128)(2,1)}, bf16[48,768]{1,0:T(8,128)(2,1)}, u32[]{:S(2)}, u32[]{:S(2)}) %collective-permute-start.20) | collective-permute-done | bytes 73760 | tf_op jit(solution)/shard_map/ppermute | solution.py:567
  171.1 4.3 %collective-permute-start.22 = (bf16[96,768]{1,0:T(8,128)(2,1)S(1)}, bf16[96,768]{1,0:T(8,128)(2,1)S(1)}, u32[]{:S(2)}, u32[]{:S(2)}) collective-permute-start(bf16[96,768]{1,0:T(8,128)(2,1)S(1)} %pad_maximum_fusion.1), channel_id=1, source_target_pairs={{0,16},{1,17},{2,18},{3,19},{4,20},{5,21},{6,22},{7,23},{8,24},{9,... | collective-permute-start | bytes 442376 | tf_op jit(solution)/shard_map/ppermute | solution.py:567
  177.9 7.2 %collective-permute-done.2 = bf16[96,2304]{1,0:T(8,128)(2,1)S(1)} collective-permute-done((bf16[96,2304]{1,0:T(8,128)(2,1)S(1)}, bf16[96,2304]{1,0:T(8,128)(2,1)S(1)}, u32[]{:S(2)}, u32[]{:S(2)}) %collective-permute-start.2) | collective-permute-done | bytes 442400 | tf_op jit(solution)/shard_map/ppermute | solution.py:567
  185.3 2.9 %collective-permute-start.5 = (bf16[24,2304]{1,0:T(8,128)(2,1)S(1)}, bf16[24,2304]{1,0:T(8,128)(2,1)S(1)}, u32[]{:S(2)}, u32[]{:S(2)}) collective-permute-start(bf16[24,2304]{1,0:T(8,128)(2,1)S(1)} %get-tuple-element.66), channel_id=1, source_target_pairs={{0,24},{1,25},{2,26},{3,27},{4,28},{5,29},{6,30},{7,31},{8,0},{9,1... | collective-permute-start | bytes 331784 | tf_op jit(solution)/shard_map/ppermute | solution.py:567
  192.3 2.6 collective-permute-start.23
  194.9 5.4 %collective-permute-done.4 = bf16[24,2304]{1,0:T(8,128)(2,1)S(1)} collective-permute-done((bf16[24,2304]{1,0:T(8,128)(2,1)S(1)}, bf16[24,2304]{1,0:T(8,128)(2,1)S(1)}, u32[]{:S(2)}, u32[]{:S(2)}) %collective-permute-start.4) | collective-permute-done | bytes 110624 | tf_op jit(solution)/shard_map/ppermute | solution.py:567
  205.7 2.9 %collective-permute-start.8 = (bf16[24,2304]{1,0:T(8,128)(2,1)S(1)}, bf16[24,2304]{1,0:T(8,128)(2,1)S(1)}, u32[]{:S(2)}, u32[]{:S(2)}) collective-permute-start(bf16[24,2304]{1,0:T(8,128)(2,1)S(1)} %get-tuple-element.64), channel_id=1, source_target_pairs={{0,24},{1,25},{2,26},{3,27},{4,28},{5,29},{6,30},{7,31},{8,0},{9,1... | collective-permute-start | bytes 331784 | tf_op jit(solution)/shard_map/ppermute | solution.py:567
  209.3 3.9 %collective-permute-done.7 = bf16[24,2304]{1,0:T(8,128)(2,1)S(1)} collective-permute-done((bf16[24,2304]{1,0:T(8,128)(2,1)S(1)}, bf16[24,2304]{1,0:T(8,128)(2,1)S(1)}, u32[]{:S(2)}, u32[]{:S(2)}) %collective-permute-start.7) | collective-permute-done | bytes 110624 | tf_op jit(solution)/shard_map/ppermute | solution.py:567
  218.2 6.6 %all-to-all-start.4 = ((bf16[32,1,16,768]{3,2,1,0:T(8,128)(2,1)}), bf16[32,1,16,768]{3,2,1,0:T(8,128)(2,1)}, u32[]{:S(2)}, u32[]{:S(2)}) async-start(bf16[32,1,16,768]{3,2,1,0:T(8,128)(2,1)} %bitcast.22), calls=%async_computation.4 | async-start | bytes 1572864 | tf_op jit(solution)/shard_map/all_to_all | solution.py:634
  231.8 2.7 %fusion.3 = bf16[256,768]{1,0:T(8,128)(2,1)} fusion(bf16[256,1536]{1,0:T(8,128)(2,1)} %get-tuple-element.44.refs_7_, bf16[768,2304]{1,0:T(8,128)(2,1)S(1)} %copy-done.1), kind=kOutput, calls=%fused_computation.8 | convolution fusion | flops 604176384 | bytes 3538944 | tf_op jit(solution)/shard_map/dot_general | solution.py:16
  236.5 8.9 %all-to-all-done.4 = bf16[32,1,16,768]{3,2,1,0:T(8,128)(2,1)} async-done(((bf16[32,1,16,768]{3,2,1,0:T(8,128)(2,1)}), bf16[32,1,16,768]{3,2,1,0:T(8,128)(2,1)}, u32[]{:S(2)}, u32[]{:S(2)}) %all-to-all-start.4) | async-done | bytes 786464 | tf_op jit(solution)/shard_map/all_to_all | solution.py:634
  245.3 3.5 %receive.1 = bf16[256,768]{1,0:T(8,128)(2,1)} custom-call(s32[32,2]{1,0:T(8,128)} %copy.29.wanted, f32[256,768]{1,0:T(8,128)} %get-tuple-element.45.own, bf16[512,768]{1,0:T(8,128)(2,1)} %bitcast.113, bf16[512,768]{1,0:T(8,128)(2,1)} %bitcast.23.second), custom_call_target="tpu_custom_call" | custom-call | tf_op jit(solution)/shard_map/receive/pallas_call | solution.py:341
  250.1 2.8 %finish.2 = f32[768,2304]{1,0:T(8,128)} custom-call(s32[1]{0:T(128)} %bitcast.25.at, bf16[192,2304]{1,0:T(8,128)(2,1)} %pad_maximum_fusion.refs_0_), custom_call_target="tpu_custom_call" | custom-call | tf_op jit(solution)/shard_map/finish/pallas_call | solution.py:524
  252.9 2.5 multiply_dynamic-update-slice_fusion.2
  255.4 2.5 multiply_dynamic-update-slice_fusion.1
  (114 shorter events, 49.8 us)
Async XLA Ops:
  19.3 30.1 %copy-start.8 = (f32[768]{0:T(1024)S(1)}, f32[768]{0:T(1024)}, u32[]{:S(2)}) copy-start(f32[768]{0:T(1024)} %param.18) | copy-start | bytes 9220
  19.3 30.7 %copy-start.9 = (f32[768]{0:T(1024)S(1)}, f32[768]{0:T(1024)}, u32[]{:S(2)}) copy-start(f32[768]{0:T(1024)} %param.19) | copy-start | bytes 9220
  19.3 31.3 %copy-start = (bf16[768,2304]{1,0:T(8,128)(2,1)S(1)}, bf16[768,2304]{1,0:T(8,128)(2,1)}, u32[]{:S(2)}) copy-start(bf16[768,2304]{1,0:T(8,128)(2,1)} %refs_2_.5) | copy-start | bytes 10616836
  45.6 41.3 %all-to-all-start.2 = ((bf16[32,1,16,768]{3,2,1,0:T(8,128)(2,1)}), bf16[32,1,16,768]{3,2,1,0:T(8,128)(2,1)}, u32[]{:S(2)}, u32[]{:S(2)}) async-start(bf16[32,1,16,768]{3,2,1,0:T(8,128)(2,1)} %bitcast.121), calls=%async_computation.2 | async-start | bytes 1572864 | tf_op jit(solution)/shard_map/all_to_all | solution.py:634
  53.3 16.6 %copy-start.10 = (s32[2,16]{1,0:T(2,128)S(1)}, s32[2,16]{1,0:T(2,128)}, u32[]{:S(2)}) copy-start(s32[2,16]{1,0:T(2,128)} %get-tuple-element.39) | copy-start | bytes 388
  109.1 12.2 %collective-permute-start.13 = (bf16[384,768]{1,0:T(8,128)(2,1)}, bf16[384,768]{1,0:T(8,128)(2,1)S(1)}, u32[]{:S(2)}, u32[]{:S(2)}) collective-permute-start(bf16[384,768]{1,0:T(8,128)(2,1)} %get-tuple-element.62), channel_id=1, source_target_pairs={{0,1},{1,0},{2,3},{3,2},{4,5},{5,4},{6,7},{7,6},{8,9},{9,8},{10,11... | collective-permute-start | bytes 1769480 | tf_op jit(solution)/shard_map/ppermute | solution.py:567
  121.1 28.0 %collective-permute-start = (bf16[384,2304]{1,0:T(8,128)(2,1)}, bf16[384,2304]{1,0:T(8,128)(2,1)S(1)}, u32[]{:S(2)}, u32[]{:S(2)}) collective-permute-start(bf16[384,2304]{1,0:T(8,128)(2,1)} %get-tuple-element.54), channel_id=1, source_target_pairs={{0,1},{1,0},{2,3},{3,2},{4,5},{5,4},{6,7},{7,6},{8,9},{9,8},{10,11... | collective-permute-start | bytes 5308424 | tf_op jit(solution)/shard_map/ppermute | solution.py:567
  122.2 8.2 %collective-permute-start.16 = (bf16[96,768]{1,0:T(8,128)(2,1)}, bf16[96,768]{1,0:T(8,128)(2,1)S(1)}, u32[]{:S(2)}, u32[]{:S(2)}) collective-permute-start(bf16[96,768]{1,0:T(8,128)(2,1)} %get-tuple-element.69), channel_id=1, source_target_pairs={{0,24},{1,25},{2,26},{3,27},{4,28},{5,29},{6,30},{7,31},{8,0},{9,1... | collective-permute-start | bytes 442376 | tf_op jit(solution)/shard_map/ppermute | solution.py:567
  125.8 13.1 %collective-permute-start.15 = (bf16[96,768]{1,0:T(8,128)(2,1)}, bf16[96,768]{1,0:T(8,128)(2,1)S(1)}, u32[]{:S(2)}, u32[]{:S(2)}) collective-permute-start(bf16[96,768]{1,0:T(8,128)(2,1)} %get-tuple-element.70), channel_id=1, source_target_pairs={{0,16},{1,17},{2,18},{3,19},{4,20},{5,21},{6,22},{7,23},{8,24},{9,... | collective-permute-start | bytes 442376 | tf_op jit(solution)/shard_map/ppermute | solution.py:567
  125.8 13.1 %collective-permute-start.14 = (bf16[96,768]{1,0:T(8,128)(2,1)}, bf16[96,768]{1,0:T(8,128)(2,1)S(1)}, u32[]{:S(2)}, u32[]{:S(2)}) collective-permute-start(bf16[96,768]{1,0:T(8,128)(2,1)} %get-tuple-element.68), channel_id=1, source_target_pairs={{0,8},{1,9},{2,10},{3,11},{4,12},{5,13},{6,14},{7,15},{8,16},{9,17... | collective-permute-start | bytes 442376 | tf_op jit(solution)/shard_map/ppermute | solution.py:567
  139.0 4.4 %collective-permute-start.17 = (bf16[48,768]{1,0:T(8,128)(2,1)S(1)}, bf16[48,768]{1,0:T(8,128)(2,1)S(1)}, u32[]{:S(2)}, u32[]{:S(2)}) collective-permute-start(bf16[48,768]{1,0:T(8,128)(2,1)S(1)} %fusion.13), channel_id=1, source_target_pairs={{0,2},{1,5},{2,0},{3,7},{4,6},{5,1},{6,4},{7,3},{8,10},{9,13},{10,... | collective-permute-start | bytes 221192 | tf_op jit(solution)/shard_map/ppermute | solution.py:567
  143.4 4.0 %collective-permute-start.18 = (bf16[24,768]{1,0:T(8,128)(2,1)S(1)}, bf16[24,768]{1,0:T(8,128)(2,1)S(1)}, u32[]{:S(2)}, u32[]{:S(2)}) collective-permute-start(bf16[24,768]{1,0:T(8,128)(2,1)S(1)} %fusion.15), channel_id=1, source_target_pairs={{0,4},{1,3},{2,6},{3,1},{4,0},{5,7},{6,2},{7,5},{8,12},{9,11},{10,... | collective-permute-start | bytes 110600 | tf_op jit(solution)/shard_map/ppermute | solution.py:567
  147.5 5.3 %collective-permute-start.19 = (bf16[24,768]{1,0:T(8,128)(2,1)S(1)}, bf16[24,768]{1,0:T(8,128)(2,1)S(1)}, u32[]{:S(2)}, u32[]{:S(2)}) collective-permute-start(bf16[24,768]{1,0:T(8,128)(2,1)S(1)} %fusion.14), channel_id=1, source_target_pairs={{0,4},{1,3},{2,6},{3,1},{4,0},{5,7},{6,2},{7,5},{8,12},{9,11},{10,... | collective-permute-start | bytes 110600 | tf_op jit(solution)/shard_map/ppermute | solution.py:567
  151.3 24.2 %collective-permute-start.1 = (bf16[192,2304]{1,0:T(8,128)(2,1)}, bf16[192,2304]{1,0:T(8,128)(2,1)}, u32[]{:S(2)}, u32[]{:S(2)}) collective-permute-start(bf16[192,2304]{1,0:T(8,128)(2,1)} %add_convert_fusion), channel_id=1, source_target_pairs={{0,2},{1,5},{2,0},{3,7},{4,6},{5,1},{6,4},{7,3},{8,10},{9,13},{10,... | collective-permute-start | bytes 2654216 | tf_op jit(solution)/shard_map/ppermute | solution.py:567
  153.4 16.7 %collective-permute-start.20 = (bf16[48,768]{1,0:T(8,128)(2,1)}, bf16[48,768]{1,0:T(8,128)(2,1)}, u32[]{:S(2)}, u32[]{:S(2)}) collective-permute-start(bf16[48,768]{1,0:T(8,128)(2,1)} %pad_maximum_fusion.2), channel_id=1, source_target_pairs={{0,2},{1,5},{2,0},{3,7},{4,6},{5,1},{6,4},{7,3},{8,10},{9,13},{10,... | collective-permute-start | bytes 221192 | tf_op jit(solution)/shard_map/ppermute | solution.py:567
  156.4 60.9 %all-to-all-start.3 = ((bf16[32,1,16,768]{3,2,1,0:T(8,128)(2,1)}), bf16[32,1,16,768]{3,2,1,0:T(8,128)(2,1)S(1)}, u32[]{:S(2)}, u32[]{:S(2)}) async-start(bf16[32,1,16,768]{3,2,1,0:T(8,128)(2,1)} %bitcast.120), calls=%async_computation.3 | async-start | bytes 1572864 | tf_op jit(solution)/shard_map/all_to_all | solution.py:634
  171.1 32.1 %collective-permute-start.21 = (bf16[96,768]{1,0:T(8,128)(2,1)S(1)}, bf16[96,768]{1,0:T(8,128)(2,1)S(1)}, u32[]{:S(2)}, u32[]{:S(2)}) collective-permute-start(bf16[96,768]{1,0:T(8,128)(2,1)S(1)} %pad_maximum_fusion.1), channel_id=1, source_target_pairs={{0,8},{1,9},{2,10},{3,11},{4,12},{5,13},{6,14},{7,15},{8,16},{9,17... | collective-permute-start | bytes 442376 | tf_op jit(solution)/shard_map/ppermute | solution.py:567
  171.1 44.8 %collective-permute-start.22 = (bf16[96,768]{1,0:T(8,128)(2,1)S(1)}, bf16[96,768]{1,0:T(8,128)(2,1)S(1)}, u32[]{:S(2)}, u32[]{:S(2)}) collective-permute-start(bf16[96,768]{1,0:T(8,128)(2,1)S(1)} %pad_maximum_fusion.1), channel_id=1, source_target_pairs={{0,16},{1,17},{2,18},{3,19},{4,20},{5,21},{6,22},{7,23},{8,24},{9,... | collective-permute-start | bytes 442376 | tf_op jit(solution)/shard_map/ppermute | solution.py:567
  176.7 8.4 %collective-permute-start.2 = (bf16[96,2304]{1,0:T(8,128)(2,1)S(1)}, bf16[96,2304]{1,0:T(8,128)(2,1)S(1)}, u32[]{:S(2)}, u32[]{:S(2)}) collective-permute-start(bf16[96,2304]{1,0:T(8,128)(2,1)S(1)} %fusion.6), channel_id=1, source_target_pairs={{0,4},{1,3},{2,6},{3,1},{4,0},{5,7},{6,2},{7,5},{8,12},{9,11},{10,... | collective-permute-start | bytes 1327112 | tf_op jit(solution)/shard_map/ppermute | solution.py:567
  185.3 7.1 %collective-permute-start.5 = (bf16[24,2304]{1,0:T(8,128)(2,1)S(1)}, bf16[24,2304]{1,0:T(8,128)(2,1)S(1)}, u32[]{:S(2)}, u32[]{:S(2)}) collective-permute-start(bf16[24,2304]{1,0:T(8,128)(2,1)S(1)} %get-tuple-element.66), channel_id=1, source_target_pairs={{0,24},{1,25},{2,26},{3,27},{4,28},{5,29},{6,30},{7,31},{8,0},{9,1... | collective-permute-start | bytes 331784 | tf_op jit(solution)/shard_map/ppermute | solution.py:567
  188.2 12.1 %collective-permute-start.4 = (bf16[24,2304]{1,0:T(8,128)(2,1)S(1)}, bf16[24,2304]{1,0:T(8,128)(2,1)S(1)}, u32[]{:S(2)}, u32[]{:S(2)}) collective-permute-start(bf16[24,2304]{1,0:T(8,128)(2,1)S(1)} %get-tuple-element.67), channel_id=1, source_target_pairs={{0,16},{1,17},{2,18},{3,19},{4,20},{5,21},{6,22},{7,23},{8,24},{9,... | collective-permute-start | bytes 331784 | tf_op jit(solution)/shard_map/ppermute | solution.py:567
  188.2 12.1 %collective-permute-start.3 = (bf16[24,2304]{1,0:T(8,128)(2,1)S(1)}, bf16[24,2304]{1,0:T(8,128)(2,1)S(1)}, u32[]{:S(2)}, u32[]{:S(2)}) collective-permute-start(bf16[24,2304]{1,0:T(8,128)(2,1)S(1)} %get-tuple-element.65), channel_id=1, source_target_pairs={{0,8},{1,9},{2,10},{3,11},{4,12},{5,13},{6,14},{7,15},{8,16},{9,17... | collective-permute-start | bytes 331784 | tf_op jit(solution)/shard_map/ppermute | solution.py:567
  192.3 24.3 %collective-permute-start.23 = (bf16[96,768]{1,0:T(8,128)(2,1)S(1)}, bf16[96,768]{1,0:T(8,128)(2,1)S(1)}, u32[]{:S(2)}, u32[]{:S(2)}) collective-permute-start(bf16[96,768]{1,0:T(8,128)(2,1)S(1)} %pad_maximum_fusion.1), channel_id=1, source_target_pairs={{0,24},{1,25},{2,26},{3,27},{4,28},{5,29},{6,30},{7,31},{8,0},{9,1... | collective-permute-start | bytes 442376 | tf_op jit(solution)/shard_map/ppermute | solution.py:567
  201.8 6.9 %collective-permute-start.6 = (bf16[24,2304]{1,0:T(8,128)(2,1)S(1)}, bf16[24,2304]{1,0:T(8,128)(2,1)S(1)}, u32[]{:S(2)}, u32[]{:S(2)}) collective-permute-start(bf16[24,2304]{1,0:T(8,128)(2,1)S(1)} %get-tuple-element.64), channel_id=1, source_target_pairs={{0,8},{1,9},{2,10},{3,11},{4,12},{5,13},{6,14},{7,15},{8,16},{9,17... | collective-permute-start | bytes 331784 | tf_op jit(solution)/shard_map/ppermute | solution.py:567
  203.8 9.4 %collective-permute-start.7 = (bf16[24,2304]{1,0:T(8,128)(2,1)S(1)}, bf16[24,2304]{1,0:T(8,128)(2,1)S(1)}, u32[]{:S(2)}, u32[]{:S(2)}) collective-permute-start(bf16[24,2304]{1,0:T(8,128)(2,1)S(1)} %get-tuple-element.64), channel_id=1, source_target_pairs={{0,16},{1,17},{2,18},{3,19},{4,20},{5,21},{6,22},{7,23},{8,24},{9,... | collective-permute-start | bytes 331784 | tf_op jit(solution)/shard_map/ppermute | solution.py:567
  205.7 8.1 %collective-permute-start.8 = (bf16[24,2304]{1,0:T(8,128)(2,1)S(1)}, bf16[24,2304]{1,0:T(8,128)(2,1)S(1)}, u32[]{:S(2)}, u32[]{:S(2)}) collective-permute-start(bf16[24,2304]{1,0:T(8,128)(2,1)S(1)} %get-tuple-element.64), channel_id=1, source_target_pairs={{0,24},{1,25},{2,26},{3,27},{4,28},{5,29},{6,30},{7,31},{8,0},{9,1... | collective-permute-start | bytes 331784 | tf_op jit(solution)/shard_map/ppermute | solution.py:567
  214.5 10.3 %collective-permute-start.9 = (bf16[96,2304]{1,0:T(8,128)(2,1)}, bf16[96,2304]{1,0:T(8,128)(2,1)}, u32[]{:S(2)}, u32[]{:S(2)}) collective-permute-start(bf16[96,2304]{1,0:T(8,128)(2,1)} %bitcast.45), channel_id=1, source_target_pairs={{0,4},{1,3},{2,6},{3,1},{4,0},{5,7},{6,2},{7,5},{8,12},{9,11},{10,... | collective-permute-start | bytes 1327112 | tf_op jit(solution)/shard_map/ppermute | solution.py:567
  217.3 31.6 %collective-permute-start.24 = (bf16[384,768]{1,0:T(8,128)(2,1)}, bf16[384,768]{1,0:T(8,128)(2,1)}, u32[]{:S(2)}, u32[]{:S(2)}) collective-permute-start(bf16[384,768]{1,0:T(8,128)(2,1)} %bitcast.65.refs_0_), channel_id=1, source_target_pairs={{0,1},{1,0},{2,3},{3,2},{4,5},{5,4},{6,7},{7,6},{8,9},{9,8},{10,11... | collective-permute-start | bytes 1769480 | tf_op jit(solution)/shard_map/ppermute | solution.py:567
  218.2 27.1 %all-to-all-start.4 = ((bf16[32,1,16,768]{3,2,1,0:T(8,128)(2,1)}), bf16[32,1,16,768]{3,2,1,0:T(8,128)(2,1)}, u32[]{:S(2)}, u32[]{:S(2)}) async-start(bf16[32,1,16,768]{3,2,1,0:T(8,128)(2,1)} %bitcast.22), calls=%async_computation.4 | async-start | bytes 1572864 | tf_op jit(solution)/shard_map/all_to_all | solution.py:634
  227.2 25.7 %collective-permute-start.10 = (bf16[192,2304]{1,0:T(8,128)(2,1)}, bf16[192,2304]{1,0:T(8,128)(2,1)}, u32[]{:S(2)}, u32[]{:S(2)}) collective-permute-start(bf16[192,2304]{1,0:T(8,128)(2,1)} %pad_maximum_fusion.refs_0_), channel_id=1, source_target_pairs={{0,1},{1,0},{2,3},{3,2},{4,5},{5,4},{6,7},{7,6},{8,9},{9,8},{10,11... | collective-permute-start | bytes 2654216 | tf_op jit(solution)/shard_map/ppermute | solution.py:567
  227.4 25.5 %collective-permute-start.11 = (bf16[192,2304]{1,0:T(8,128)(2,1)}, bf16[192,2304]{1,0:T(8,128)(2,1)}, u32[]{:S(2)}, u32[]{:S(2)}) collective-permute-start(bf16[192,2304]{1,0:T(8,128)(2,1)} %pad_maximum_fusion.refs_0_), channel_id=1, source_target_pairs={{0,2},{1,5},{2,0},{3,7},{4,6},{5,1},{6,4},{7,3},{8,10},{9,13},{10,... | collective-permute-start | bytes 2654216 | tf_op jit(solution)/shard_map/ppermute | solution.py:567
  252.8 5.0 %collective-permute-start.12 = (bf16[192,2304]{1,0:T(8,128)(2,1)}, bf16[192,2304]{1,0:T(8,128)(2,1)S(1)}, u32[]{:S(2)}, u32[]{:S(2)}) collective-permute-start(bf16[192,2304]{1,0:T(8,128)(2,1)} %collective-permute-done.11), channel_id=1, source_target_pairs={{0,1},{1,0},{2,3},{3,2},{4,5},{5,4},{6,7},{7,6},{8,9},{9,8},{10,11... | collective-permute-start | bytes 2654216 | tf_op jit(solution)/shard_map/ppermute | solution.py:567
  (8 other events, 59.0 us)
